TPU v7x, 512 devices: a whole 4x4x16 slice. The times are simulated.
512 devices in a mesh: row: 32 (over z, x_lo), col: 16 (over x_hi, y, core).
Axes of the slice: x: 4 (x_hi: 2, x_lo: 2; x = x_hi * 2 + x_lo), y: 4, z: 16, core: 2. Of those that a mesh axis runs over, the one named last changes fastest.
Arguments:
- stereo_neuron_outputs: bfloat16 [2, 256, 64, 2048], P(None, 'row', None, 'col'), may hold values from -6 to 6
- filter_tap_coefficients: bfloat16 [3, 3, 3, 64, 64], replicated, may hold values from -0.25 to 0.25
- filter_stack_intercepts: float32 [3, 64], replicated, may hold values from -3 to 3
- reference_picture_present: int32 [256, 2048], P('row', 'col'), may hold values 0 or 1
- tile_shift_amounts: int32 [32, 16], P('row', 'col'), may hold values from 0 to 256, as said below
- smoothness_charges: int32 [2], replicated, may hold values from 4 to 96, as said below
Outputs:
- aggregated: float32 [256, 2048, 128], P('row', 'col')
Inputs may be any that keep to these rules, and one draw needn't show every extreme that they name: `tile_shift_amounts`: every tile's offset is a whole number of 0 to 256; some tile has exactly 256. smoothness_charges[0] lies in 4 to 16; smoothness_charges[1] is 96.
All inputs are finite; a program needn't handle non-finite values. No bound on the sum of `reference_picture_present` on one device may be relied on, other than what follows from the above.
Results may differ from a plain program's by a relative error of at most 0.006.
Values may be sent and summed in bfloat16 or wider, within the bound.
A program may use at most 64 MiB of HBM per device.

v0:
```python
import jax
import jax.numpy as jnp
from jax import lax
from jax.sharding import PartitionSpec as P

DISPARITIES = 128
BLOCKS = 2


def from_behind(block, axis, distance):
    devices = range(lax.axis_size(axis))
    route = [(i - distance, i) for i in devices if i - distance in devices]
    return lax.ppermute(block, axis, route)


def extended_2(value, sides, width):
    for axis, dim in sides:
        count, length = (lax.axis_size(axis), value.shape[dim])
        up = [(i, (i + 1) % count) for i in range(count - 1)]
        down = [(j, i) for i, j in up]
        last = lax.slice_in_dim(value, length - width, length, axis=dim)
        first = lax.slice_in_dim(value, 0, width, axis=dim)
        before = lax.ppermute(last, axis, up)
        after = lax.ppermute(first, axis, down)
        value = jnp.concatenate([before, value, after], axis=dim)
    return value


def advance(state, cost_row, gentle_change_charge, steep_change_charge):
    least = jnp.min(state, axis=-1, keepdims=True)
    barrier = jnp.full(state.shape[:-1] + (1,), jnp.inf, state.dtype)
    lower = jnp.concatenate([barrier, state[..., :-1]], axis=-1)
    upper = jnp.concatenate([state[..., 1:], barrier], axis=-1)
    best = jnp.minimum(
        jnp.minimum(state, jnp.minimum(lower, upper) + gentle_change_charge),
        least + steep_change_charge,
    )
    return cost_row + best - least


def sweep(costs, incoming, gentle_change_charge, steep_change_charge, backward):

    def stepper(state, cost_row):
        fresh = advance(state, cost_row, gentle_change_charge, steep_change_charge)
        return (fresh, fresh)

    return lax.scan(stepper, incoming, costs, reverse=backward)


def block_pass(block, incoming, backward, costs, total, gentle_change_charge, steep_change_charge):
    width = incoming.shape[0]
    count = costs.shape[1] // width
    inside = jnp.logical_and(block >= 0, block < count)
    start = jnp.clip(block, 0, count - 1) * width

    def work(current):
        piece = lax.dynamic_slice_in_dim(costs, start, width, 1)
        final, layers = sweep(piece, incoming, gentle_change_charge, steep_change_charge, backward)
        before = lax.dynamic_slice_in_dim(current, start, width, 1)
        return (final, lax.dynamic_update_slice_in_dim(current, before + layers, start, 1))

    def skip(current):
        return (incoming, current)

    return lax.cond(inside, work, skip, total)


def pass_down_rows(edge, offset_by):
    return from_behind(edge.astype(jnp.bfloat16), "row", offset_by).astype(edge.dtype)


def pass_across_cols(edge, offset_by):
    return from_behind(edge, "col", offset_by)


def vertical_turn(turn, carry, costs, gentle_change_charge, steep_change_charge):
    down_sent, up_sent, total = carry
    down_in = pass_down_rows(down_sent, 1)
    up_in = pass_down_rows(up_sent, -1)
    rank = lax.axis_index("row")
    extent = lax.axis_size("row")
    down_out, total = block_pass(
        turn - rank, down_in, False, costs, total, gentle_change_charge, steep_change_charge
    )
    up_out, total = block_pass(
        turn - (extent - 1 - rank),
        up_in,
        True,
        costs,
        total,
        gentle_change_charge,
        steep_change_charge,
    )
    return (down_out, up_out, total)


def horizontal_turn(turn, carry, costs, gentle_change_charge, steep_change_charge):
    right_sent, left_outgoing_message, total = carry
    right_in = pass_across_cols(right_sent, 1)
    left_in = pass_across_cols(left_outgoing_message, -1)
    rank = lax.axis_index("col")
    extent = lax.axis_size("col")
    right_out, total = block_pass(
        turn - rank, right_in, False, costs, total, gentle_change_charge, steep_change_charge
    )
    left_out, total = block_pass(
        turn - (extent - 1 - rank),
        left_in,
        True,
        costs,
        total,
        gentle_change_charge,
        steep_change_charge,
    )
    return (right_out, left_out, total)


def conv_stack(stereo_neuron_outputs, filter_tap_coefficients, filter_stack_intercepts):
    layers_total = filter_tap_coefficients.shape[0]
    rows_here = stereo_neuron_outputs.shape[1]
    cols_here = stereo_neuron_outputs.shape[3]
    hidden = extended_2(stereo_neuron_outputs, (("row", 1), ("col", 3)), layers_total)
    row_start = lax.axis_index("row") * rows_here
    col_start = lax.axis_index("col") * cols_here
    row_limit = lax.axis_size("row") * rows_here
    col_limit = lax.axis_size("col") * cols_here
    features = None
    for layer_number in range(layers_total):
        margin = layers_total - 1 - layer_number
        out_rows = rows_here + 2 * margin
        out_cols = cols_here + 2 * margin
        summed = None
        for tap_row in range(3):
            for tap_col in range(3):
                window = hidden[:, tap_row : tap_row + out_rows, :, tap_col : tap_col + out_cols]
                term = jnp.einsum(
                    "oc,iycx->iyox",
                    filter_tap_coefficients[layer_number, tap_row, tap_col],
                    window,
                    preferred_element_type=jnp.float32,
                )
                summed = term if summed is None else summed + term
        summed = summed + filter_stack_intercepts[layer_number][None, None, :, None]
        if layer_number < layers_total - 1:
            global_rows = row_start - margin + jnp.arange(out_rows, dtype=jnp.int32)
            global_cols = col_start - margin + jnp.arange(out_cols, dtype=jnp.int32)
            keep_rows = jnp.logical_and(global_rows >= 0, global_rows < row_limit)
            keep_cols = jnp.logical_and(global_cols >= 0, global_cols < col_limit)
            keeper = jnp.logical_and(keep_rows[None, :, None, None], keep_cols[None, None, None, :])
            hidden = jnp.where(keeper, jnp.maximum(summed, 0.0), 0.0).astype(jnp.bfloat16)
        else:
            features = summed
    scale = lax.rsqrt(jnp.sum(features * features, axis=2, keepdims=True) + 1e-06)
    return (features * scale).astype(jnp.bfloat16)


def per_device(
    stereo_neuron_outputs,
    filter_tap_coefficients,
    filter_stack_intercepts,
    reference_picture_present,
    tile_shift_amounts,
    smoothness_charges,
):
    unit = conv_stack(stereo_neuron_outputs, filter_tap_coefficients, filter_stack_intercepts)
    left_unit = unit[0]
    right_normalized_features = unit[1]
    rows_here = left_unit.shape[0]
    cols_here = left_unit.shape[2]
    reach = (3 * cols_here + DISPARITIES - 2) // cols_here
    tile_offset = tile_shift_amounts[0, 0]
    pieces = [
        from_behind(right_normalized_features, "col", distance) for distance in range(reach, 0, -1)
    ]
    extended = jnp.concatenate(pieces + [right_normalized_features], axis=2)
    strip_start = reach * cols_here - tile_offset - (DISPARITIES - 1)
    strip = lax.dynamic_slice_in_dim(extended, strip_start, cols_here + DISPARITIES - 1, 2)
    product = jnp.einsum("ycj,yck->yjk", left_unit, strip, preferred_element_type=jnp.float32)
    padded = jnp.pad(product, ((0, 0), (0, 0), (0, 1)))
    flat = padded.reshape(rows_here, cols_here * (cols_here + DISPARITIES))
    flat = jnp.pad(flat, ((0, 0), (0, cols_here)))
    skewed = flat.reshape(rows_here, cols_here, cols_here + DISPARITIES + 1)[:, :, :DISPARITIES]
    similarity = skewed[:, :, ::-1]
    cost = jnp.where(reference_picture_present[:, :, None] == 1, 1.0 - similarity, 1.0)
    gentle_change_charge = smoothness_charges[0].astype(jnp.float32) / 64.0
    steep_change_charge = smoothness_charges[1].astype(jnp.float32) / 64.0
    across = jnp.swapaxes(cost, 0, 1)
    column_edge = jnp.zeros((cols_here // BLOCKS, DISPARITIES), jnp.float32)
    row_edge = jnp.zeros((rows_here // BLOCKS, DISPARITIES), jnp.float32)
    start_vertical = (column_edge, column_edge, jnp.zeros_like(cost))
    start_horizontal = (row_edge, row_edge, jnp.zeros_like(across))
    vertical_done = lax.fori_loop(
        0,
        lax.axis_size("row") + BLOCKS - 1,
        lambda turn, carry: vertical_turn(
            turn, carry, cost, gentle_change_charge, steep_change_charge
        ),
        start_vertical,
    )
    horizontal_done = lax.fori_loop(
        0,
        lax.axis_size("col") + BLOCKS - 1,
        lambda turn, carry: horizontal_turn(
            turn, carry, across, gentle_change_charge, steep_change_charge
        ),
        start_horizontal,
    )
    vertical = vertical_done[2]
    horizontal = horizontal_done[2]
    return vertical + jnp.swapaxes(horizontal, 0, 1)


def solution(mesh):
    return jax.shard_map(
        per_device,
        mesh=mesh,
        in_specs=(P(None, "row", None, "col"), P(), P(), P("row", "col"), P("row", "col"), P()),
        out_specs=P("row", "col", None),
        check_vma=False,
    )
```

profile of v0, /device:TPU:2, one launch (start us, length us, event | category | flops | bytes accessed | tf_op | source)
XLA Modules:
  0.0 1245.0 jit_solution(5661020110386979296)
XLA Ops:
  4.8 5.3 collective-permute-start.5
  30.5 8.4 collective-permute-start.10
  51.9 787.1 %while.91 = (s32[]{:T(128)}, f32[4,128]{1,0:T(4,128)S(1)}, f32[4,128]{1,0:T(4,128)S(1)}, f32[128,8,128]{2,1,0:T(8,128)S(1)}, f32[128,8,128]{2,1,0:T(8,128)S(1)},...) while((s32[]{:T(128)}, f32[4,128]{1,0:T(4,128)S(1)}, ...), condition=%wide.region_24.25_spmd, body=%wide.region_13.24_spmd.sunk | while | flops 138272 | bytes 2956247 | solution.py:200
  51.9 6.7 collective-permute-start
  60.0 37.1 %conditional.10 = ((f32[4,128]{1,0:T(4,128)S(1)}, f32[128,8,128]{2,1,0:T(8,128)S(1)})) conditional(s32[]{:T(128)} %convert_element_type.108, (f32[4,128]{1,0:T(4,128)S(1)}, f32[128,8,128]{2,1,0:T(8,128)S(1)}) %tuple.201, (s32[]{:T(128)}, f32[128,8,128]{2,1,0:T(8,128)S(1)}, f32[]{:T(128)}, f32[]{:T(128)}, f32[4,128]{1,0:T(4,128)S(1)}, ...), branch_computations={%region_14.14_spmd, %region_15.18_spmd} | conditional | flops 69128 | bytes 1334531 | solution.py:65
  60.0 36.9 %while.88 = (s32[]{:T(128)}, f32[4,128]{1,0:T(4,128)S(1)}, f32[128,4,128]{2,1,0:T(4,128)S(1)}, f32[128,4,128]{2,1,0:T(4,128)S(1)}, f32[]{:T(128)}, /*index=5*/f32[]{:T(128)}, s32[]{:T(128)}, f32[]{:T(128)}) while((s32[]{:T(128)}, f32[4,128]{1,0:T(4,128)S(1)}, f32[128,4,128]{2,1,0:T(4,128)S(1)}, f32[128,4,128]{2,1,0:T(4,128)S(1)}, ...), condition=%wide.region_18.17_spmd, body=%wide.region_16.16_spmd.sunk | while | flops 3586 | bytes 23637 | solution.py:47
  99.8 37.1 %conditional.10 = ((f32[4,128]{1,0:T(4,128)S(1)}, f32[128,8,128]{2,1,0:T(8,128)S(1)})) conditional(s32[]{:T(128)} %convert_element_type.108, (f32[4,128]{1,0:T(4,128)S(1)}, f32[128,8,128]{2,1,0:T(8,128)S(1)}) %tuple.201, (s32[]{:T(128)}, f32[128,8,128]{2,1,0:T(8,128)S(1)}, f32[]{:T(128)}, f32[]{:T(128)}, f32[4,128]{1,0:T(4,128)S(1)}, ...), branch_computations={%region_14.14_spmd, %region_15.18_spmd} | conditional | flops 69128 | bytes 1334531 | solution.py:65
  99.9 36.9 %while.88 = (s32[]{:T(128)}, f32[4,128]{1,0:T(4,128)S(1)}, f32[128,4,128]{2,1,0:T(4,128)S(1)}, f32[128,4,128]{2,1,0:T(4,128)S(1)}, f32[]{:T(128)}, /*index=5*/f32[]{:T(128)}, s32[]{:T(128)}, f32[]{:T(128)}) while((s32[]{:T(128)}, f32[4,128]{1,0:T(4,128)S(1)}, f32[128,4,128]{2,1,0:T(4,128)S(1)}, f32[128,4,128]{2,1,0:T(4,128)S(1)}, ...), condition=%wide.region_18.17_spmd, body=%wide.region_16.16_spmd.sunk | while | flops 3586 | bytes 23637 | solution.py:47
  143.1 38.5 %collective-permute-start = (f32[4,128]{1,0:T(4,128)S(1)}, f32[4,128]{1,0:T(4,128)S(1)}, u32[]{:S(2)}, u32[]{:S(2)}) collective-permute-start(f32[4,128]{1,0:T(4,128)S(1)} %get-tuple-element.1346), channel_id=1, source_target_pairs={{0,1},{1,2},{2,3},{3,4},{4,5},{5,6},{6,7},{7,8},{8,9},{9,10},{10,1... | collective-permute-start | bytes 6152 | tf_op jit(solution)/shard_map/while/body/eval_jaxpr/ppermute | solution.py:13
  185.5 4.2 collective-permute-start
  191.1 37.2 %collective-permute-done.1 = f32[4,128]{1,0:T(4,128)S(1)} collective-permute-done((f32[4,128]{1,0:T(4,128)S(1)}, f32[4,128]{1,0:T(4,128)S(1)}, u32[]{:S(2)}, u32[]{:S(2)}) %collective-permute-start.1) | collective-permute-done | bytes 2080 | tf_op jit(solution)/shard_map/while/body/eval_jaxpr/ppermute | solution.py:13
  228.3 4.2 collective-permute-start
  235.6 36.8 %collective-permute-start = (f32[4,128]{1,0:T(4,128)S(1)}, f32[4,128]{1,0:T(4,128)S(1)}, u32[]{:S(2)}, u32[]{:S(2)}) collective-permute-start(f32[4,128]{1,0:T(4,128)S(1)} %get-tuple-element.1346), channel_id=1, source_target_pairs={{0,1},{1,2},{2,3},{3,4},{4,5},{5,6},{6,7},{7,8},{8,9},{9,10},{10,1... | collective-permute-start | bytes 6152 | tf_op jit(solution)/shard_map/while/body/eval_jaxpr/ppermute | solution.py:13
  280.6 36.6 %collective-permute-done.1 = f32[4,128]{1,0:T(4,128)S(1)} collective-permute-done((f32[4,128]{1,0:T(4,128)S(1)}, f32[4,128]{1,0:T(4,128)S(1)}, u32[]{:S(2)}, u32[]{:S(2)}) %collective-permute-start.1) | collective-permute-done | bytes 2080 | tf_op jit(solution)/shard_map/while/body/eval_jaxpr/ppermute | solution.py:13
  317.2 4.8 collective-permute-start
  325.1 36.8 %collective-permute-start = (f32[4,128]{1,0:T(4,128)S(1)}, f32[4,128]{1,0:T(4,128)S(1)}, u32[]{:S(2)}, u32[]{:S(2)}) collective-permute-start(f32[4,128]{1,0:T(4,128)S(1)} %get-tuple-element.1346), channel_id=1, source_target_pairs={{0,1},{1,2},{2,3},{3,4},{4,5},{5,6},{6,7},{7,8},{8,9},{9,10},{10,1... | collective-permute-start | bytes 6152 | tf_op jit(solution)/shard_map/while/body/eval_jaxpr/ppermute | solution.py:13
  370.1 36.0 %collective-permute-done.1 = f32[4,128]{1,0:T(4,128)S(1)} collective-permute-done((f32[4,128]{1,0:T(4,128)S(1)}, f32[4,128]{1,0:T(4,128)S(1)}, u32[]{:S(2)}, u32[]{:S(2)}) %collective-permute-start.1) | collective-permute-done | bytes 2080 | tf_op jit(solution)/shard_map/while/body/eval_jaxpr/ppermute | solution.py:13
  406.1 5.5 collective-permute-start
  412.9 11.6 collective-permute-done.1
  424.5 77.5 %collective-permute-start = (f32[4,128]{1,0:T(4,128)S(1)}, f32[4,128]{1,0:T(4,128)S(1)}, u32[]{:S(2)}, u32[]{:S(2)}) collective-permute-start(f32[4,128]{1,0:T(4,128)S(1)} %get-tuple-element.1346), channel_id=1, source_target_pairs={{0,1},{1,2},{2,3},{3,4},{4,5},{5,6},{6,7},{7,8},{8,9},{9,10},{10,1... | collective-permute-start | bytes 6152 | tf_op jit(solution)/shard_map/while/body/eval_jaxpr/ppermute | solution.py:13
  503.4 41.9 %collective-permute-done.1 = f32[4,128]{1,0:T(4,128)S(1)} collective-permute-done((f32[4,128]{1,0:T(4,128)S(1)}, f32[4,128]{1,0:T(4,128)S(1)}, u32[]{:S(2)}, u32[]{:S(2)}) %collective-permute-start.1) | collective-permute-done | bytes 2080 | tf_op jit(solution)/shard_map/while/body/eval_jaxpr/ppermute | solution.py:13
  545.3 46.9 %collective-permute-start = (f32[4,128]{1,0:T(4,128)S(1)}, f32[4,128]{1,0:T(4,128)S(1)}, u32[]{:S(2)}, u32[]{:S(2)}) collective-permute-start(f32[4,128]{1,0:T(4,128)S(1)} %get-tuple-element.1346), channel_id=1, source_target_pairs={{0,1},{1,2},{2,3},{3,4},{4,5},{5,6},{6,7},{7,8},{8,9},{9,10},{10,1... | collective-permute-start | bytes 6152 | tf_op jit(solution)/shard_map/while/body/eval_jaxpr/ppermute | solution.py:13
  593.6 37.8 %collective-permute-done.1 = f32[4,128]{1,0:T(4,128)S(1)} collective-permute-done((f32[4,128]{1,0:T(4,128)S(1)}, f32[4,128]{1,0:T(4,128)S(1)}, u32[]{:S(2)}, u32[]{:S(2)}) %collective-permute-start.1) | collective-permute-done | bytes 2080 | tf_op jit(solution)/shard_map/while/body/eval_jaxpr/ppermute | solution.py:13
  631.4 42.0 %collective-permute-start = (f32[4,128]{1,0:T(4,128)S(1)}, f32[4,128]{1,0:T(4,128)S(1)}, u32[]{:S(2)}, u32[]{:S(2)}) collective-permute-start(f32[4,128]{1,0:T(4,128)S(1)} %get-tuple-element.1346), channel_id=1, source_target_pairs={{0,1},{1,2},{2,3},{3,4},{4,5},{5,6},{6,7},{7,8},{8,9},{9,10},{10,1... | collective-permute-start | bytes 6152 | tf_op jit(solution)/shard_map/while/body/eval_jaxpr/ppermute | solution.py:13
  674.8 38.5 %collective-permute-done.1 = f32[4,128]{1,0:T(4,128)S(1)} collective-permute-done((f32[4,128]{1,0:T(4,128)S(1)}, f32[4,128]{1,0:T(4,128)S(1)}, u32[]{:S(2)}, u32[]{:S(2)}) %collective-permute-start.1) | collective-permute-done | bytes 2080 | tf_op jit(solution)/shard_map/while/body/eval_jaxpr/ppermute | solution.py:13
  713.3 41.4 %collective-permute-start = (f32[4,128]{1,0:T(4,128)S(1)}, f32[4,128]{1,0:T(4,128)S(1)}, u32[]{:S(2)}, u32[]{:S(2)}) collective-permute-start(f32[4,128]{1,0:T(4,128)S(1)} %get-tuple-element.1346), channel_id=1, source_target_pairs={{0,1},{1,2},{2,3},{3,4},{4,5},{5,6},{6,7},{7,8},{8,9},{9,10},{10,1... | collective-permute-start | bytes 6152 | tf_op jit(solution)/shard_map/while/body/eval_jaxpr/ppermute | solution.py:13
  757.8 37.1 %conditional.11 = ((f32[4,128]{1,0:T(4,128)S(1)}, f32[128,8,128]{2,1,0:T(8,128)S(1)})) conditional(s32[]{:T(128)} %convert_element_type.109, (f32[4,128]{1,0:T(4,128)S(1)}, f32[128,8,128]{2,1,0:T(8,128)S(1)}) %tuple.203, (s32[]{:T(128)}, f32[128,8,128]{2,1,0:T(8,128)S(1)}, f32[]{:T(128)}, f32[]{:T(128)}, f32[4,128]{1,0:T(4,128)S(1)}, ...), branch_computations={%region_19.19_spmd, %region_20.23_spmd} | conditional | flops 69129 | bytes 1596707 | solution.py:65
  757.9 36.9 %while.89 = (s32[]{:T(128)}, f32[4,128]{1,0:T(4,128)S(1)}, f32[128,4,128]{2,1,0:T(4,128)S(1)}, f32[128,4,128]{2,1,0:T(4,128)S(1)}, f32[]{:T(128)}, /*index=5*/f32[]{:T(128)}, s32[]{:T(128)}, s32[]{:T(128)}, f32[]{:T(128)}) while((s32[]{:T(128)}, f32[4,128]{1,0:T(4,128)S(1)}, f32[128,4,128]{2,1,0:T(4,128)S(1)}, ...), condition=%wide.region_23.22_spmd, body=%wide.region_21.21_spmd.sunk | while | flops 3587 | bytes 23657 | solution.py:47
  801.9 37.1 %conditional.11 = ((f32[4,128]{1,0:T(4,128)S(1)}, f32[128,8,128]{2,1,0:T(8,128)S(1)})) conditional(s32[]{:T(128)} %convert_element_type.109, (f32[4,128]{1,0:T(4,128)S(1)}, f32[128,8,128]{2,1,0:T(8,128)S(1)}) %tuple.203, (s32[]{:T(128)}, f32[128,8,128]{2,1,0:T(8,128)S(1)}, f32[]{:T(128)}, f32[]{:T(128)}, f32[4,128]{1,0:T(4,128)S(1)}, ...), branch_computations={%region_19.19_spmd, %region_20.23_spmd} | conditional | flops 69129 | bytes 1596707 | solution.py:65
  802.0 36.9 %while.89 = (s32[]{:T(128)}, f32[4,128]{1,0:T(4,128)S(1)}, f32[128,4,128]{2,1,0:T(4,128)S(1)}, f32[128,4,128]{2,1,0:T(4,128)S(1)}, f32[]{:T(128)}, /*index=5*/f32[]{:T(128)}, s32[]{:T(128)}, s32[]{:T(128)}, f32[]{:T(128)}) while((s32[]{:T(128)}, f32[4,128]{1,0:T(4,128)S(1)}, f32[128,4,128]{2,1,0:T(4,128)S(1)}, ...), condition=%wide.region_23.22_spmd, body=%wide.region_21.21_spmd.sunk | while | flops 3587 | bytes 23657 | solution.py:47
  839.1 405.0 %while.90 = (s32[]{:T(128)}, f32[64,128]{1,0:T(8,128)S(1)}, f32[64,128]{1,0:T(8,128)S(1)}, f32[8,128,128]{2,1,0:T(8,128)S(1)}, f32[8,128,128]{2,1,0:T(8,128)S(1)...) while((s32[]{:T(128)}, f32[64,128]{1,0:T(8,128)S(1)}, ...), condition=%wide.region_12.13_spmd, body=%wide.region_1.12_spmd.sunk | while | flops 294817 | bytes 3999763 | solution.py:192
  874.3 4.5 collective-permute-done.3
  884.8 4.5 collective-permute-done.3
  895.3 4.5 collective-permute-done.3
  905.8 4.5 collective-permute-done.3
  965.1 4.7 collective-permute-done.3
  975.7 4.9 collective-permute-done.3
  986.6 4.5 collective-permute-done.3
  997.1 4.5 collective-permute-done.3
  1007.6 4.5 collective-permute-done.3
  1037.5 5.1 collective-permute-done.3
  1042.6 6.8 collective-permute-start.2
  1051.4 7.2 collective-permute-done.3
  1058.7 6.7 collective-permute-start.2
  1067.4 7.3 collective-permute-done.3
  1074.7 6.9 collective-permute-start.2
  1083.6 7.2 collective-permute-done.3
  1090.8 6.7 collective-permute-start.2
  1099.6 8.6 collective-permute-done.3
  1108.2 6.7 collective-permute-start.2
  1116.9 7.7 collective-permute-done.3
  1124.6 6.7 collective-permute-start.2
  1133.3 7.3 collective-permute-done.3
  1140.7 6.7 collective-permute-start.2
  1149.4 7.3 collective-permute-done.3
  1156.8 6.7 collective-permute-start.2
  1165.5 8.5 collective-permute-done.3
  1174.1 6.7 collective-permute-start.2
  1182.8 7.3 collective-permute-done.3
  1190.1 6.7 collective-permute-start.2
  1198.9 7.3 collective-permute-done.3
  1206.2 6.7 collective-permute-start.2
  1215.0 4.5 collective-permute-done.3
  1228.3 4.5 collective-permute-done.3
  (2730 shorter events, 447.9 us)
Async XLA Ops:
  1.0 11.9 collective-permute-start.4
  4.8 9.1 collective-permute-start.5
  30.5 14.9 %collective-permute-start.10 = (bf16[8,64,128]{2,1,0:T(8,128)(2,1)S(1)}, bf16[8,64,128]{2,1,0:T(8,128)(2,1)S(1)}, u32[]{:S(2)}, u32[]{:S(2)}) collective-permute-start(bf16[8,64,128]{2,1,0:T(8,128)(2,1)S(1)} %slice_bitcast_fusion), channel_id=1, source_target_pairs={{0,1},{1,2},{2,3},{3,4},{4,5},{5,6},{6,7},{7,8},{8,9},{9,10},{10,1... | collective-permute-start | bytes 393224 | tf_op jit(solution)/shard_map/ppermute | solution.py:13
  51.9 8.0 collective-permute-start
  58.6 38.5 %collective-permute-start.1 = (f32[4,128]{1,0:T(4,128)S(1)}, f32[4,128]{1,0:T(4,128)S(1)}, u32[]{:S(2)}, u32[]{:S(2)}) collective-permute-start(f32[4,128]{1,0:T(4,128)S(1)} %get-tuple-element.1347), channel_id=1, source_target_pairs={{1,0},{2,1},{3,2},{4,3},{5,4},{6,5},{7,6},{8,7},{9,8},{10,9},{11,1... | collective-permute-start | bytes 6152 | tf_op jit(solution)/shard_map/while/body/eval_jaxpr/ppermute | solution.py:13
  98.5 38.5 %collective-permute-start.1 = (f32[4,128]{1,0:T(4,128)S(1)}, f32[4,128]{1,0:T(4,128)S(1)}, u32[]{:S(2)}, u32[]{:S(2)}) collective-permute-start(f32[4,128]{1,0:T(4,128)S(1)} %get-tuple-element.1347), channel_id=1, source_target_pairs={{1,0},{2,1},{3,2},{4,3},{5,4},{6,5},{7,6},{8,7},{9,8},{10,9},{11,1... | collective-permute-start | bytes 6152 | tf_op jit(solution)/shard_map/while/body/eval_jaxpr/ppermute | solution.py:13
  143.1 39.8 %collective-permute-start = (f32[4,128]{1,0:T(4,128)S(1)}, f32[4,128]{1,0:T(4,128)S(1)}, u32[]{:S(2)}, u32[]{:S(2)}) collective-permute-start(f32[4,128]{1,0:T(4,128)S(1)} %get-tuple-element.1346), channel_id=1, source_target_pairs={{0,1},{1,2},{2,3},{3,4},{4,5},{5,6},{6,7},{7,8},{8,9},{9,10},{10,1... | collective-permute-start | bytes 6152 | tf_op jit(solution)/shard_map/while/body/eval_jaxpr/ppermute | solution.py:13
  189.7 38.6 %collective-permute-start.1 = (f32[4,128]{1,0:T(4,128)S(1)}, f32[4,128]{1,0:T(4,128)S(1)}, u32[]{:S(2)}, u32[]{:S(2)}) collective-permute-start(f32[4,128]{1,0:T(4,128)S(1)} %get-tuple-element.1347), channel_id=1, source_target_pairs={{1,0},{2,1},{3,2},{4,3},{5,4},{6,5},{7,6},{8,7},{9,8},{10,9},{11,1... | collective-permute-start | bytes 6152 | tf_op jit(solution)/shard_map/while/body/eval_jaxpr/ppermute | solution.py:13
  235.6 38.1 %collective-permute-start = (f32[4,128]{1,0:T(4,128)S(1)}, f32[4,128]{1,0:T(4,128)S(1)}, u32[]{:S(2)}, u32[]{:S(2)}) collective-permute-start(f32[4,128]{1,0:T(4,128)S(1)} %get-tuple-element.1346), channel_id=1, source_target_pairs={{0,1},{1,2},{2,3},{3,4},{4,5},{5,6},{6,7},{7,8},{8,9},{9,10},{10,1... | collective-permute-start | bytes 6152 | tf_op jit(solution)/shard_map/while/body/eval_jaxpr/ppermute | solution.py:13
  279.3 37.9 %collective-permute-start.1 = (f32[4,128]{1,0:T(4,128)S(1)}, f32[4,128]{1,0:T(4,128)S(1)}, u32[]{:S(2)}, u32[]{:S(2)}) collective-permute-start(f32[4,128]{1,0:T(4,128)S(1)} %get-tuple-element.1347), channel_id=1, source_target_pairs={{1,0},{2,1},{3,2},{4,3},{5,4},{6,5},{7,6},{8,7},{9,8},{10,9},{11,1... | collective-permute-start | bytes 6152 | tf_op jit(solution)/shard_map/while/body/eval_jaxpr/ppermute | solution.py:13
  325.1 38.1 %collective-permute-start = (f32[4,128]{1,0:T(4,128)S(1)}, f32[4,128]{1,0:T(4,128)S(1)}, u32[]{:S(2)}, u32[]{:S(2)}) collective-permute-start(f32[4,128]{1,0:T(4,128)S(1)} %get-tuple-element.1346), channel_id=1, source_target_pairs={{0,1},{1,2},{2,3},{3,4},{4,5},{5,6},{6,7},{7,8},{8,9},{9,10},{10,1... | collective-permute-start | bytes 6152 | tf_op jit(solution)/shard_map/while/body/eval_jaxpr/ppermute | solution.py:13
  368.8 37.3 %collective-permute-start.1 = (f32[4,128]{1,0:T(4,128)S(1)}, f32[4,128]{1,0:T(4,128)S(1)}, u32[]{:S(2)}, u32[]{:S(2)}) collective-permute-start(f32[4,128]{1,0:T(4,128)S(1)} %get-tuple-element.1347), channel_id=1, source_target_pairs={{1,0},{2,1},{3,2},{4,3},{5,4},{6,5},{7,6},{8,7},{9,8},{10,9},{11,1... | collective-permute-start | bytes 6152 | tf_op jit(solution)/shard_map/while/body/eval_jaxpr/ppermute | solution.py:13
  406.1 6.8 collective-permute-start
  411.6 13.0 %collective-permute-start.1 = (f32[4,128]{1,0:T(4,128)S(1)}, f32[4,128]{1,0:T(4,128)S(1)}, u32[]{:S(2)}, u32[]{:S(2)}) collective-permute-start(f32[4,128]{1,0:T(4,128)S(1)} %get-tuple-element.1347), channel_id=1, source_target_pairs={{1,0},{2,1},{3,2},{4,3},{5,4},{6,5},{7,6},{8,7},{9,8},{10,9},{11,1... | collective-permute-start | bytes 6152 | tf_op jit(solution)/shard_map/while/body/eval_jaxpr/ppermute | solution.py:13
  424.5 78.8 %collective-permute-start = (f32[4,128]{1,0:T(4,128)S(1)}, f32[4,128]{1,0:T(4,128)S(1)}, u32[]{:S(2)}, u32[]{:S(2)}) collective-permute-start(f32[4,128]{1,0:T(4,128)S(1)} %get-tuple-element.1346), channel_id=1, source_target_pairs={{0,1},{1,2},{2,3},{3,4},{4,5},{5,6},{6,7},{7,8},{8,9},{9,10},{10,1... | collective-permute-start | bytes 6152 | tf_op jit(solution)/shard_map/while/body/eval_jaxpr/ppermute | solution.py:13
  502.1 43.3 %collective-permute-start.1 = (f32[4,128]{1,0:T(4,128)S(1)}, f32[4,128]{1,0:T(4,128)S(1)}, u32[]{:S(2)}, u32[]{:S(2)}) collective-permute-start(f32[4,128]{1,0:T(4,128)S(1)} %get-tuple-element.1347), channel_id=1, source_target_pairs={{1,0},{2,1},{3,2},{4,3},{5,4},{6,5},{7,6},{8,7},{9,8},{10,9},{11,1... | collective-permute-start | bytes 6152 | tf_op jit(solution)/shard_map/while/body/eval_jaxpr/ppermute | solution.py:13
  545.3 48.2 %collective-permute-start = (f32[4,128]{1,0:T(4,128)S(1)}, f32[4,128]{1,0:T(4,128)S(1)}, u32[]{:S(2)}, u32[]{:S(2)}) collective-permute-start(f32[4,128]{1,0:T(4,128)S(1)} %get-tuple-element.1346), channel_id=1, source_target_pairs={{0,1},{1,2},{2,3},{3,4},{4,5},{5,6},{6,7},{7,8},{8,9},{9,10},{10,1... | collective-permute-start | bytes 6152 | tf_op jit(solution)/shard_map/while/body/eval_jaxpr/ppermute | solution.py:13
  592.2 39.2 %collective-permute-start.1 = (f32[4,128]{1,0:T(4,128)S(1)}, f32[4,128]{1,0:T(4,128)S(1)}, u32[]{:S(2)}, u32[]{:S(2)}) collective-permute-start(f32[4,128]{1,0:T(4,128)S(1)} %get-tuple-element.1347), channel_id=1, source_target_pairs={{1,0},{2,1},{3,2},{4,3},{5,4},{6,5},{7,6},{8,7},{9,8},{10,9},{11,1... | collective-permute-start | bytes 6152 | tf_op jit(solution)/shard_map/while/body/eval_jaxpr/ppermute | solution.py:13
  631.4 43.4 %collective-permute-start = (f32[4,128]{1,0:T(4,128)S(1)}, f32[4,128]{1,0:T(4,128)S(1)}, u32[]{:S(2)}, u32[]{:S(2)}) collective-permute-start(f32[4,128]{1,0:T(4,128)S(1)} %get-tuple-element.1346), channel_id=1, source_target_pairs={{0,1},{1,2},{2,3},{3,4},{4,5},{5,6},{6,7},{7,8},{8,9},{9,10},{10,1... | collective-permute-start | bytes 6152 | tf_op jit(solution)/shard_map/while/body/eval_jaxpr/ppermute | solution.py:13
  673.5 39.8 %collective-permute-start.1 = (f32[4,128]{1,0:T(4,128)S(1)}, f32[4,128]{1,0:T(4,128)S(1)}, u32[]{:S(2)}, u32[]{:S(2)}) collective-permute-start(f32[4,128]{1,0:T(4,128)S(1)} %get-tuple-element.1347), channel_id=1, source_target_pairs={{1,0},{2,1},{3,2},{4,3},{5,4},{6,5},{7,6},{8,7},{9,8},{10,9},{11,1... | collective-permute-start | bytes 6152 | tf_op jit(solution)/shard_map/while/body/eval_jaxpr/ppermute | solution.py:13
  713.3 42.8 %collective-permute-start = (f32[4,128]{1,0:T(4,128)S(1)}, f32[4,128]{1,0:T(4,128)S(1)}, u32[]{:S(2)}, u32[]{:S(2)}) collective-permute-start(f32[4,128]{1,0:T(4,128)S(1)} %get-tuple-element.1346), channel_id=1, source_target_pairs={{0,1},{1,2},{2,3},{3,4},{4,5},{5,6},{6,7},{7,8},{8,9},{9,10},{10,1... | collective-permute-start | bytes 6152 | tf_op jit(solution)/shard_map/while/body/eval_jaxpr/ppermute | solution.py:13
  842.1 6.5 collective-permute-start.3
  852.1 6.5 collective-permute-start.3
  861.7 6.7 collective-permute-start.3
  872.3 6.5 collective-permute-start.3
  882.8 6.5 collective-permute-start.3
  893.3 6.5 collective-permute-start.3
  903.8 6.5 collective-permute-start.3
  913.5 6.5 collective-permute-start.3
  923.3 6.5 collective-permute-start.3
  932.9 6.5 collective-permute-start.3
  942.6 6.5 collective-permute-start.3
  952.6 6.5 collective-permute-start.3
  963.0 6.7 collective-permute-start.3
  973.7 6.9 collective-permute-start.3
  984.6 6.5 collective-permute-start.3
  995.1 6.5 collective-permute-start.3
  1005.6 6.5 collective-permute-start.3
  1025.0 6.5 collective-permute-start.3
  1034.7 7.9 collective-permute-start.3
  1042.6 8.7 collective-permute-start.2
  1049.4 9.2 collective-permute-start.3
  1058.7 8.7 collective-permute-start.2
  1065.4 9.3 collective-permute-start.3
  1074.7 8.9 collective-permute-start.2
  1081.6 9.2 collective-permute-start.3
  1090.8 8.7 collective-permute-start.2
  1097.6 10.6 collective-permute-start.3
  1108.2 8.7 collective-permute-start.2
  1114.9 9.7 collective-permute-start.3
  1124.6 8.7 collective-permute-start.2
  1131.3 9.3 collective-permute-start.3
  1140.7 8.7 collective-permute-start.2
  1147.4 9.3 collective-permute-start.3
  1156.8 8.7 collective-permute-start.2
  1163.5 10.5 collective-permute-start.3
  1174.1 8.7 collective-permute-start.2
  1180.8 9.3 collective-permute-start.3
  1190.1 8.7 collective-permute-start.2
  1196.9 9.3 collective-permute-start.3
  1206.2 8.7 collective-permute-start.2
  1213.0 6.5 collective-permute-start.3
  1226.3 6.5 collective-permute-start.3
  1237.5 6.5 collective-permute-start.3
  (46 other events, 261.0 us)
where the time goes:
time: 1250 us; the launch traced here: 1240 us
  starting transfers between devices  634 us (51%)
  waiting for transfers between devices  424 us (34%)
  other arithmetic  114 us (9%)
  local copies, waits for them, and re-layouts  47.2 us (4%)
    ppermute x103, starting transfers between devices, from_behind(): return lax.ppermute(block, axis, route)  622 us
    ppermute x103, waiting for transfers between devices, from_behind(): return lax.ppermute(block, axis, route)  423 us
    reduce_min x548, other arithmetic, advance(): least = jnp.min(state, axis=-1, keepdims=True)  68.7 us
    dynamic_update_slice x512, other arithmetic, sweep(): return lax.scan(stepper, incoming, costs, reverse=backward)  39.6 us
    slice x544, local copies, waits for them, and re-layouts, advance(): lower = jnp.concatenate([barrier, state[..., :-1]], axis=-1)  39.6 us
  transfers between devices with their start and end apart: 107, of which 50 were waited for; matrix products, arithmetic and copies ran while one was open for 6% of the time, Pallas kernels for 0%

commit v1 on v0

v1 whole, which is shorter than its diff:
```python
import functools

import jax
import jax.numpy as jnp
from jax import lax
from jax.experimental import pallas as pl
from jax.experimental.pallas import tpu as pltpu
from jax.sharding import PartitionSpec as P

DISPARITIES = 128
SUB = 8
PARTS = DISPARITIES // SUB
MESH = pl.DeviceIdType.MESH


def from_behind(block, axis, distance):
    devices = range(lax.axis_size(axis))
    route = [(i - distance, i) for i in devices if i - distance in devices]
    return lax.ppermute(block, axis, route)


def extended_2(value, sides, width):
    for axis, dim in sides:
        count, length = (lax.axis_size(axis), value.shape[dim])
        up = [(i, (i + 1) % count) for i in range(count - 1)]
        down = [(j, i) for i, j in up]
        last = lax.slice_in_dim(value, length - width, length, axis=dim)
        first = lax.slice_in_dim(value, 0, width, axis=dim)
        before = lax.ppermute(last, axis, up)
        after = lax.ppermute(first, axis, down)
        value = jnp.concatenate([before, value, after], axis=dim)
    return value


def lane_order():
    lane = lax.broadcasted_iota(jnp.int32, (SUB, DISPARITIES), 1)
    return (lane % SUB) * PARTS + lane // SUB


def lane_order_back():
    lane = lax.broadcasted_iota(jnp.int32, (SUB, DISPARITIES), 1)
    return (lane % PARTS) * SUB + lane // PARTS


def pieces_of(value):
    return [value[v * SUB : (v + 1) * SUB] for v in range(PARTS)]


def smallest(state):
    level = list(state)
    while len(level) > 1:
        level = [jnp.minimum(level[2 * i], level[2 * i + 1]) for i in range(len(level) // 2)]
    least = level[0]
    for step in (4, 2, 1):
        least = jnp.minimum(least, pltpu.roll(least, step, 0))
    return least


def step_once(state, cost, p1, p2, first_sub, last_sub):
    lifted = [s + p1 for s in state]
    below = jnp.where(first_sub, jnp.inf, pltpu.roll(lifted[-1], 1, 0))
    above = jnp.where(last_sub, jnp.inf, pltpu.roll(lifted[0], SUB - 1, 0))
    near = [below] + lifted + [above]
    jump = smallest(state) + p2
    return [
        cost[v]
        + jnp.minimum(jnp.minimum(state[v], jnp.minimum(near[v], near[v + 2])), jump)
        for v in range(PARTS)
    ]


def walk(slots, out, count, state, charges, at):
    sub = lax.broadcasted_iota(jnp.int32, (SUB, SUB), 0)
    first_sub, last_sub = sub == 0, sub == SUB - 1
    p1 = charges[0].astype(jnp.float32) / 64.0
    p2 = charges[1].astype(jnp.float32) / 64.0

    def body(turn, state):
        state = list(state)
        for k in range(8):
            t = at(turn * 8 + k)
            state = step_once(state, pieces_of(slots[t]), p1, p2, first_sub, last_sub)
            for v in range(PARTS):
                out[t, v * SUB : (v + 1) * SUB, :] = state[v]
        return tuple(state)

    return list(lax.fori_loop(0, count // 8, body, tuple(state)))


def turn_in(source, slots, count):
    order = lane_order()

    def body(turn, _):
        for k in range(8):
            t = turn * 8 + k
            slots[t] = jnp.take_along_axis(source[t], order, axis=1).T
        return 0

    lax.fori_loop(0, count // 8, body, 0)


def vertical_kernel(source, charges, out, slots):
    count = source.shape[0]
    turn_in(source, slots, count)
    zero = [jnp.zeros((SUB, SUB), jnp.float32) for _ in range(PARTS)]
    walk(slots, slots, count, zero, charges, lambda t: t)
    back = lane_order_back()

    def body(turn, least):
        for k in range(8):
            t = turn * 8 + k
            value = slots[t].T
            out[t] = jnp.take_along_axis(value - least, back, axis=1)
            least = jnp.min(value, axis=1, keepdims=True)
        return least

    lax.fori_loop(0, count // 8, body, jnp.zeros((SUB, 1), jnp.float32))


def vertical_call(source, charges):
    count = source.shape[0]
    return pl.pallas_call(
        vertical_kernel,
        out_shape=jax.ShapeDtypeStruct(source.shape, jnp.float32),
        in_specs=[
            pl.BlockSpec(memory_space=pltpu.VMEM),
            pl.BlockSpec(memory_space=pltpu.SMEM),
        ],
        out_specs=pl.BlockSpec(memory_space=pltpu.VMEM),
        scratch_shapes=[pltpu.VMEM((count, DISPARITIES, SUB), jnp.float32)],
        name="vertical_paths",
    )(source, charges)


def horizontal_kernel(
    size, source, charges, out, slots, walked, edge_out, edge_in, send_sem, recv_sem
):
    count = source.shape[0]
    me = lax.axis_index("col")
    barrier = pltpu.get_barrier_semaphore()

    @pl.when(me > 0)
    def _():
        pl.semaphore_signal(barrier, inc=1, device_id={"col": me - 1}, device_id_type=MESH)

    @pl.when(me < size - 1)
    def _():
        pl.semaphore_signal(barrier, inc=1, device_id={"col": me + 1}, device_id_type=MESH)

    neighbours = jnp.where(me > 0, 1, 0) + jnp.where(me < size - 1, 1, 0)
    pl.semaphore_wait(barrier, neighbours)

    turn_in(source, slots, count)
    back = lane_order_back()

    def one_direction(way, first):
        starts = me == (0 if way == 0 else size - 1)
        ends = me == (size - 1 if way == 0 else 0)
        toward = me + 1 if way == 0 else me - 1
        at = (lambda t: t) if way == 0 else (lambda t: count - 1 - t)

        def copy():
            return pltpu.make_async_remote_copy(
                src_ref=edge_out.at[way],
                dst_ref=edge_in.at[way],
                send_sem=send_sem.at[way],
                recv_sem=recv_sem.at[way],
                device_id={"col": toward},
                device_id_type=MESH,
            )

        @pl.when(starts)
        def _():
            edge_in[way] = jnp.zeros((SUB, DISPARITIES), jnp.float32)

        @pl.when(jnp.logical_not(starts))
        def _():
            copy().wait_recv()

        edge = edge_in[way]
        state = walk(slots, walked, count, pieces_of(edge.T), charges, at)
        last = jnp.concatenate(state, axis=0).T

        @pl.when(jnp.logical_not(ends))
        def _():
            edge_out[way] = last - jnp.min(last, axis=1, keepdims=True)
            copy().start()

        def body(turn, least):
            for k in range(8):
                t = at(turn * 8 + k)
                value = walked[t].T
                result = jnp.take_along_axis(value - least, back, axis=1)
                out[t] = result if first else out[t] + result
                least = jnp.min(value, axis=1, keepdims=True)
            return least

        lax.fori_loop(0, count // 8, body, jnp.min(edge, axis=1, keepdims=True))

        @pl.when(jnp.logical_not(ends))
        def _():
            copy().wait_send()

    @pl.when(me < size // 2)
    def _():
        one_direction(0, True)
        one_direction(1, False)

    @pl.when(me >= size // 2)
    def _():
        one_direction(1, True)
        one_direction(0, False)


def horizontal_call(source, charges):
    count = source.shape[0]
    size = lax.axis_size("col")
    return pl.pallas_call(
        functools.partial(horizontal_kernel, size),
        out_shape=jax.ShapeDtypeStruct(source.shape, jnp.float32),
        in_specs=[
            pl.BlockSpec(memory_space=pltpu.VMEM),
            pl.BlockSpec(memory_space=pltpu.SMEM),
        ],
        out_specs=pl.BlockSpec(memory_space=pltpu.VMEM),
        scratch_shapes=[
            pltpu.VMEM((count, DISPARITIES, SUB), jnp.float32),
            pltpu.VMEM((count, DISPARITIES, SUB), jnp.float32),
            pltpu.VMEM((2, SUB, DISPARITIES), jnp.float32),
            pltpu.VMEM((2, SUB, DISPARITIES), jnp.float32),
            pltpu.SemaphoreType.DMA((2,)),
            pltpu.SemaphoreType.DMA((2,)),
        ],
        compiler_params=pltpu.CompilerParams(collective_id=0, has_side_effects=True),
        name="horizontal_paths",
    )(source, charges)


def conv_stack(stereo_neuron_outputs, filter_tap_coefficients, filter_stack_intercepts):
    layers_total = filter_tap_coefficients.shape[0]
    rows_here = stereo_neuron_outputs.shape[1]
    cols_here = stereo_neuron_outputs.shape[3]
    hidden = extended_2(stereo_neuron_outputs, (("row", 1), ("col", 3)), layers_total)
    row_start = lax.axis_index("row") * rows_here
    col_start = lax.axis_index("col") * cols_here
    row_limit = lax.axis_size("row") * rows_here
    col_limit = lax.axis_size("col") * cols_here
    features = None
    for layer_number in range(layers_total):
        margin = layers_total - 1 - layer_number
        out_rows = rows_here + 2 * margin
        out_cols = cols_here + 2 * margin
        summed = None
        for tap_row in range(3):
            for tap_col in range(3):
                window = hidden[:, tap_row : tap_row + out_rows, :, tap_col : tap_col + out_cols]
                term = jnp.einsum(
                    "oc,iycx->iyox",
                    filter_tap_coefficients[layer_number, tap_row, tap_col],
                    window,
                    preferred_element_type=jnp.float32,
                )
                summed = term if summed is None else summed + term
        summed = summed + filter_stack_intercepts[layer_number][None, None, :, None]
        if layer_number < layers_total - 1:
            global_rows = row_start - margin + jnp.arange(out_rows, dtype=jnp.int32)
            global_cols = col_start - margin + jnp.arange(out_cols, dtype=jnp.int32)
            keep_rows = jnp.logical_and(global_rows >= 0, global_rows < row_limit)
            keep_cols = jnp.logical_and(global_cols >= 0, global_cols < col_limit)
            keeper = jnp.logical_and(keep_rows[None, :, None, None], keep_cols[None, None, None, :])
            hidden = jnp.where(keeper, jnp.maximum(summed, 0.0), 0.0).astype(jnp.bfloat16)
        else:
            features = summed
    scale = lax.rsqrt(jnp.sum(features * features, axis=2, keepdims=True) + 1e-06)
    return (features * scale).astype(jnp.bfloat16)


def per_device(
    stereo_neuron_outputs,
    filter_tap_coefficients,
    filter_stack_intercepts,
    reference_picture_present,
    tile_shift_amounts,
    smoothness_charges,
):
    unit = conv_stack(stereo_neuron_outputs, filter_tap_coefficients, filter_stack_intercepts)
    left_unit = unit[0]
    right_normalized_features = unit[1]
    rows_here = left_unit.shape[0]
    cols_here = left_unit.shape[2]
    reach = (3 * cols_here + DISPARITIES - 2) // cols_here
    tile_offset = tile_shift_amounts[0, 0]
    pieces = [
        from_behind(right_normalized_features, "col", distance) for distance in range(reach, 0, -1)
    ]
    extended = jnp.concatenate(pieces + [right_normalized_features], axis=2)
    strip_start = reach * cols_here - tile_offset - (DISPARITIES - 1)
    strip = lax.dynamic_slice_in_dim(extended, strip_start, cols_here + DISPARITIES - 1, 2)
    product = jnp.einsum("ycj,yck->yjk", left_unit, strip, preferred_element_type=jnp.float32)
    padded = jnp.pad(product, ((0, 0), (0, 0), (0, 1)))
    flat = padded.reshape(rows_here, cols_here * (cols_here + DISPARITIES))
    flat = jnp.pad(flat, ((0, 0), (0, cols_here)))
    skewed = flat.reshape(rows_here, cols_here, cols_here + DISPARITIES + 1)[:, :, :DISPARITIES]
    similarity = skewed[:, :, ::-1]
    cost = jnp.where(reference_picture_present[:, :, None] == 1, 1.0 - similarity, 1.0)
    horizontal = horizontal_call(jnp.swapaxes(cost, 0, 1), smoothness_charges)
    strip = lax.all_to_all(
        cost.astype(jnp.bfloat16), "row", split_axis=1, concat_axis=0, tiled=True
    ).astype(jnp.float32)
    width = strip.shape[1]
    both = vertical_call(jnp.concatenate([strip, strip[::-1]], axis=1), smoothness_charges)
    vertical = (both[:, :width] + both[::-1, width:]).astype(jnp.bfloat16)
    vertical = lax.all_to_all(vertical, "row", split_axis=0, concat_axis=1, tiled=True)
    return vertical.astype(jnp.float32) + jnp.swapaxes(horizontal, 0, 1)


def solution(mesh):
    return jax.shard_map(
        per_device,
        mesh=mesh,
        in_specs=(P(None, "row", None, "col"), P(), P(), P("row", "col"), P("row", "col"), P()),
        out_specs=P("row", "col", None),
        check_vma=False,
    )
```

time: 1250 us -> 226 us (0.18)
  starting transfers between devices: 634 us -> 31.1 us
  waiting for transfers between devices: 424 us -> 5.8 us
  Pallas kernels: 0 us -> 129 us
  other arithmetic: 114 us -> 6.28 us
  local copies, waits for them, and re-layouts: 47.2 us -> 7.45 us
  blocking collectives: 0 us -> 33.7 us
    ppermute x103 -> x3, starting transfers between devices: 622 us -> 14.4 us  [from_behind(): return lax.ppermute(block, axis, route)]
    ppermute x103 -> x3, waiting for transfers between devices: 423 us -> 1.4 us  [from_behind(): return lax.ppermute(block, axis, route)]
    pallas_call x0 -> x2, Pallas kernels: none -> 129 us  [the longest x1 94.5 us: horizontal_call(): pl.pallas_call(functools.partial(horizontal_kernel, size), out_shape=jax....]
    reduce_min x548 -> x0, other arithmetic: 68.7 us -> none  [advance(): least = jnp.min(state, axis=-1, keepdims=True)]
    dynamic_update_slice x520 -> x0, other arithmetic: 40.3 us -> none  [the longest x512 39.6 us: sweep(): return lax.scan(stepper, incoming, costs, reverse=backward)]
    slice x545 -> x1, local copies, waits for them, and re-layouts: 40.2 us -> 1.34 us  [per_device(): vertical = (both[:, :width] + both[::-1, width:]).astype(jnp.bfloat16)]
    all_to_all x0 -> x1, blocking collectives: none -> 33.7 us  [per_device(): lax.all_to_all(cost.astype(jnp.bfloat16), 'row', split_axis=1, concat_axi...]
  transfers between devices with their start and end apart: 107 -> 8, of which waited for: 50 -> 3; matrix products, arithmetic and copies ran while one was open for 6% -> 1% of each run, Pallas kernels for 0% -> 42%
where the time goes in v1:
time: 226 us
  Pallas kernels  129 us (57%)
  blocking collectives  33.7 us (15%)
  starting transfers between devices  31.1 us (14%)
  matrix products  10.6 us (5%)
  local copies, waits for them, and re-layouts  7.45 us (3%)
  other arithmetic  6.28 us (3%)
  waiting for transfers between devices  5.8 us (3%)
    pallas_call x1, Pallas kernels, horizontal_call(): pl.pallas_call(functools.partial(horizontal_kernel, size), out_shape=jax....  94.5 us
    pallas_call x1, Pallas kernels, vertical_call(): pl.pallas_call(vertical_kernel, out_shape=jax.ShapeDtypeStruct(source.sha...  34.9 us
    all_to_all x1, blocking collectives, per_device(): lax.all_to_all(cost.astype(jnp.bfloat16), 'row', split_axis=1, concat_axi...  33.7 us
    ppermute x3, starting transfers between devices, from_behind(): return lax.ppermute(block, axis, route)  14.4 us
    dot_general x27, matrix products, conv_stack(): jnp.einsum('oc,iycx->iyox', filter_tap_coefficients[layer_number, tap_row...  10.1 us
    ppermute x2, starting transfers between devices, extended_2(): after = lax.ppermute(first, axis, down)  6.58 us
    ppermute x2, starting transfers between devices, extended_2(): before = lax.ppermute(last, axis, up)  5.25 us
    all_to_all x1, starting transfers between devices, per_device(): lax.all_to_all(vertical, 'row', split_axis=0, concat_axis=1, tiled=True)  4.87 us
  transfers between devices with their start and end apart: 8, of which 3 were waited for; matrix products, arithmetic and copies ran while one was open for 1% of the time, Pallas kernels for 42%

profile of v1, /device:TPU:2, one launch (start us, length us, event | category | flops | bytes accessed | tf_op | source)
XLA Modules:
  0.0 225.5 jit_solution(12171162465219112386)
XLA Ops:
  0.0 1.0 fusion.115
  1.0 3.8 %collective-permute-start = (bf16[2,3,64,128]{3,2,1,0:T(8,128)(2,1)S(1)}, bf16[2,3,64,128]{3,2,1,0:T(8,128)(2,1)S(1)}, u32[]{:S(2)}, u32[]{:S(2)}) collective-permute-start(bf16[2,3,64,128]{3,2,1,0:T(8,128)(2,1)S(1)} %get-tuple-element.10), channel_id=1, source_target_pairs={{0,16},{16,32},{32,48},{48,64},{64,80},{80,96},{96,112},{112,128},... | collective-permute-start | bytes 294920 | tf_op jit(solution)/shard_map/ppermute | solution.py:29
  4.8 5.3 %collective-permute-start.1 = (bf16[2,3,64,128]{3,2,1,0:T(8,128)(2,1)S(1)}, bf16[2,3,64,128]{3,2,1,0:T(8,128)(2,1)S(1)}, u32[]{:S(2)}, u32[]{:S(2)}) collective-permute-start(bf16[2,3,64,128]{3,2,1,0:T(8,128)(2,1)S(1)} %get-tuple-element.9), channel_id=1, source_target_pairs={{16,0},{32,16},{48,32},{64,48},{80,64},{96,80},{112,96},{128,112},... | collective-permute-start | bytes 294920 | tf_op jit(solution)/shard_map/ppermute | solution.py:30
  10.1 0.1 broadcast_and_fusion
  10.2 0.1 broadcast_and_fusion.1
  10.3 2.5 %collective-permute-done = bf16[2,3,64,128]{3,2,1,0:T(8,128)(2,1)S(1)} collective-permute-done((bf16[2,3,64,128]{3,2,1,0:T(8,128)(2,1)S(1)}, bf16[2,3,64,128]{3,2,1,0:T(8,128)(2,1)S(1)}, u32[]{:S(2)}, u32[]{:S(2)}) %collective-permute-start) | collective-permute-done | bytes 98336 | tf_op jit(solution)/shard_map/ppermute | solution.py:29
  12.8 1.0 constant_dynamic-update-slice_fusion.1
  13.9 0.2 fusion.114
  14.1 1.4 collective-permute-start.2
  15.6 1.3 collective-permute-start.3
  17.5 1.9 collective-permute-done.3
  19.4 0.6 pad_maximum_fusion.1
  20.0 0.4 fusion.13
  20.4 0.3 fusion.15
  20.8 0.4 fusion.17
  21.2 0.4 fusion.19
  21.6 0.3 fusion.21
  22.0 0.4 fusion.23
  22.4 0.4 fusion.25
  22.9 0.3 fusion.27
  23.2 1.1 fusion.10
  24.4 0.3 fusion.37
  24.7 0.4 convolution_add_fusion.7
  25.1 0.4 convolution_add_fusion.6
  25.5 0.3 convolution_add_fusion.5
  25.8 0.4 convolution_add_fusion.4
  26.2 0.4 convolution_add_fusion.3
  26.6 0.3 convolution_add_fusion.2
  26.9 0.4 convolution_add_fusion.1
  27.3 0.4 fusion.4
  27.8 0.2 fusion.56
  28.0 0.3 convolution_add_fusion.15
  28.3 0.3 convolution_add_fusion.14
  28.6 0.2 convolution_add_fusion.13
  28.8 0.3 convolution_add_fusion.12
  29.1 0.3 convolution_add_fusion.11
  29.4 0.2 convolution_add_fusion.10
  29.6 0.3 convolution_add_fusion.9
  29.9 0.3 multiply_reduce_fusion
  30.3 0.1 fusion.42
  30.4 9.7 %collective-permute-start.4 = (bf16[8,64,128]{2,1,0:T(8,128)(2,1)S(1)}, bf16[8,64,128]{2,1,0:T(8,128)(2,1)S(1)}, u32[]{:S(2)}, u32[]{:S(2)}) collective-permute-start(bf16[8,64,128]{2,1,0:T(8,128)(2,1)S(1)} %slice_bitcast_fusion), channel_id=1, source_target_pairs={{0,3},{1,4},{2,5},{3,6},{4,7},{5,8},{6,9},{7,10},{8,11},{9,12},{10... | collective-permute-start | bytes 393224 | tf_op jit(solution)/shard_map/ppermute | solution.py:19
  40.1 3.2 %collective-permute-start.5 = (bf16[8,64,128]{2,1,0:T(8,128)(2,1)S(1)}, bf16[8,64,128]{2,1,0:T(8,128)(2,1)S(1)}, u32[]{:S(2)}, u32[]{:S(2)}) collective-permute-start(bf16[8,64,128]{2,1,0:T(8,128)(2,1)S(1)} %slice_bitcast_fusion), channel_id=1, source_target_pairs={{0,2},{1,3},{2,4},{3,5},{4,6},{5,7},{6,8},{7,9},{8,10},{9,11},{10,... | collective-permute-start | bytes 393224 | tf_op jit(solution)/shard_map/ppermute | solution.py:19
  43.3 1.5 collective-permute-start.6
  44.8 0.1 copy.11
  44.9 1.4 collective-permute-done.5
  46.3 0.6 fusion.46
  46.9 0.1 pad_bitcast_fusion
  47.0 0.6 copy.44
  47.6 0.1 pad.9
  47.7 1.3 reshape.124
  49.0 0.3 copy.43
  49.3 0.2 rev.9
  49.5 1.0 fusion.40
  50.5 33.7 %all_to_all.8 = bf16[8,128,128]{2,0,1:T(8,128)(2,1)S(1)} all-to-all(bf16[8,128,128]{2,0,1:T(8,128)(2,1)S(1)} %get-tuple-element.6), channel_id=1, replica_groups=mesh['row'=32,'col'=16] {'row'}, dimensions={1} | all-to-all | bytes 524288 | tf_op jit(solution)/shard_map/all_to_all | solution.py:307
  84.3 0.1 copy.13
  84.4 0.1 rev.10
  84.5 1.2 pad_maximum_fusion.source
  85.7 34.9 %vertical_paths.1 = f32[256,8,128]{2,1,0:T(8,128)} custom-call(f32[256,8,128]{2,1,0:T(8,128)} %pad_maximum_fusion.source, s32[2]{0:T(128)} %charges.3), custom_call_target="tpu_custom_call" | custom-call | tf_op jit(solution)/shard_map/vertical_paths/pallas_call | solution.py:122
  120.6 1.3 slice.297
  121.9 2.1 fusion.39
  124.0 4.9 %all-to-all-start.1 = ((bf16[256,4,128]{2,1,0:T(4,128)(2,1)}), bf16[256,4,128]{2,1,0:T(4,128)(2,1)S(1)}, u32[]{:S(2)}, u32[]{:S(2)}) async-start(bf16[256,4,128]{2,1,0:T(4,128)(2,1)} %fusion.39), calls=%async_computation.1 | async-start | bytes 524288 | tf_op jit(solution)/shard_map/all_to_all | solution.py:313
  128.9 94.5 %horizontal_paths.1 = f32[128,8,128]{2,1,0:T(8,128)} custom-call(f32[128,8,128]{2,1,0:T(8,128)} %get-tuple-element.5.source, s32[2]{0:T(128)} %charges.3), custom_call_target="tpu_custom_call" | custom-call | tf_op jit(solution)/shard_map/horizontal_paths/pallas_call | solution.py:218
  223.5 1.1 bitcast_add_fusion
  224.6 0.9 copy.15
  (24 shorter events, 0.3 us)
Async XLA Ops:
  0.0 16.9 %copy-start.2 = (f32[3,64]{1,0:T(4,128)S(1)}, f32[3,64]{1,0:T(4,128)}, u32[]{:S(2)}) copy-start(f32[3,64]{1,0:T(4,128)} %param.8) | copy-start | bytes 2308
  1.0 11.9 %collective-permute-start = (bf16[2,3,64,128]{3,2,1,0:T(8,128)(2,1)S(1)}, bf16[2,3,64,128]{3,2,1,0:T(8,128)(2,1)S(1)}, u32[]{:S(2)}, u32[]{:S(2)}) collective-permute-start(bf16[2,3,64,128]{3,2,1,0:T(8,128)(2,1)S(1)} %get-tuple-element.10), channel_id=1, source_target_pairs={{0,16},{16,32},{32,48},{48,64},{64,80},{80,96},{96,112},{112,128},... | collective-permute-start | bytes 294920 | tf_op jit(solution)/shard_map/ppermute | solution.py:29
  4.8 9.1 %collective-permute-start.1 = (bf16[2,3,64,128]{3,2,1,0:T(8,128)(2,1)S(1)}, bf16[2,3,64,128]{3,2,1,0:T(8,128)(2,1)S(1)}, u32[]{:S(2)}, u32[]{:S(2)}) collective-permute-start(bf16[2,3,64,128]{3,2,1,0:T(8,128)(2,1)S(1)} %get-tuple-element.9), channel_id=1, source_target_pairs={{16,0},{32,16},{48,32},{64,48},{80,64},{96,80},{112,96},{128,112},... | collective-permute-start | bytes 294920 | tf_op jit(solution)/shard_map/ppermute | solution.py:30
  14.1 5.9 %copy-start = (bf16[3,3,3,64,64]{4,3,2,1,0:T(8,128)(2,1)S(1)}, bf16[3,3,3,64,64]{4,3,2,1,0:T(8,128)(2,1)}, u32[]{:S(2)}) copy-start(bf16[3,3,3,64,64]{4,3,2,1,0:T(8,128)(2,1)} %param.7) | copy-start | bytes 663556
  14.1 3.4 %collective-permute-start.2 = (bf16[2,14,64,3]{3,2,1,0:T(8,128)(2,1)S(1)}, bf16[2,14,64,3]{3,2,1,0:T(8,128)(2,1)S(1)}, u32[]{:S(2)}, u32[]{:S(2)}) collective-permute-start(bf16[2,14,64,3]{3,2,1,0:T(8,128)(2,1)S(1)} %get-tuple-element.7), channel_id=1, source_target_pairs={{0,1},{1,2},{2,3},{3,4},{4,5},{5,6},{6,7},{7,8},{8,9},{9,10},{10,1... | collective-permute-start | bytes 32264 | tf_op jit(solution)/shard_map/ppermute | solution.py:29
  15.6 3.8 %collective-permute-start.3 = (bf16[2,14,64,3]{3,2,1,0:T(8,128)(2,1)S(1)}, bf16[2,14,64,3]{3,2,1,0:T(8,128)(2,1)S(1)}, u32[]{:S(2)}, u32[]{:S(2)}) collective-permute-start(bf16[2,14,64,3]{3,2,1,0:T(8,128)(2,1)S(1)} %get-tuple-element.8), channel_id=1, source_target_pairs={{1,0},{2,1},{3,2},{4,3},{5,4},{6,5},{7,6},{8,7},{9,8},{10,9},{11,1... | collective-permute-start | bytes 32264 | tf_op jit(solution)/shard_map/ppermute | solution.py:30
  29.6 15.1 %copy-start.1 = (s32[8,128]{1,0:T(8,128)S(1)}, s32[8,128]{1,0:T(8,128)}, u32[]{:S(2)}) copy-start(s32[8,128]{1,0:T(8,128)} %param.9) | copy-start | bytes 12292
  30.4 14.5 %collective-permute-start.4 = (bf16[8,64,128]{2,1,0:T(8,128)(2,1)S(1)}, bf16[8,64,128]{2,1,0:T(8,128)(2,1)S(1)}, u32[]{:S(2)}, u32[]{:S(2)}) collective-permute-start(bf16[8,64,128]{2,1,0:T(8,128)(2,1)S(1)} %slice_bitcast_fusion), channel_id=1, source_target_pairs={{0,3},{1,4},{2,5},{3,6},{4,7},{5,8},{6,9},{7,10},{8,11},{9,12},{10... | collective-permute-start | bytes 393224 | tf_op jit(solution)/shard_map/ppermute | solution.py:19
  40.1 6.2 %collective-permute-start.5 = (bf16[8,64,128]{2,1,0:T(8,128)(2,1)S(1)}, bf16[8,64,128]{2,1,0:T(8,128)(2,1)S(1)}, u32[]{:S(2)}, u32[]{:S(2)}) collective-permute-start(bf16[8,64,128]{2,1,0:T(8,128)(2,1)S(1)} %slice_bitcast_fusion), channel_id=1, source_target_pairs={{0,2},{1,3},{2,4},{3,5},{4,6},{5,7},{6,8},{7,9},{8,10},{9,11},{10,... | collective-permute-start | bytes 393224 | tf_op jit(solution)/shard_map/ppermute | solution.py:19
  43.3 3.0 %collective-permute-start.6 = (bf16[8,64,128]{2,1,0:T(8,128)(2,1)S(1)}, bf16[8,64,128]{2,1,0:T(8,128)(2,1)S(1)}, u32[]{:S(2)}, u32[]{:S(2)}) collective-permute-start(bf16[8,64,128]{2,1,0:T(8,128)(2,1)S(1)} %slice_bitcast_fusion), channel_id=1, source_target_pairs={{0,1},{1,2},{2,3},{3,4},{4,5},{5,6},{6,7},{7,8},{8,9},{9,10},{10,1... | collective-permute-start | bytes 393224 | tf_op jit(solution)/shard_map/ppermute | solution.py:19
  124.0 99.4 %all-to-all-start.1 = ((bf16[256,4,128]{2,1,0:T(4,128)(2,1)}), bf16[256,4,128]{2,1,0:T(4,128)(2,1)S(1)}, u32[]{:S(2)}, u32[]{:S(2)}) async-start(bf16[256,4,128]{2,1,0:T(4,128)(2,1)} %fusion.39), calls=%async_computation.1 | async-start | bytes 524288 | tf_op jit(solution)/shard_map/all_to_all | solution.py:313

commit v2 on v1

--- a/solution.py
+++ b/solution.py
@@ -87,75 +87,164 @@
     return list(lax.fori_loop(0, count // 8, body, tuple(state)))
 
 
-def turn_in(source, slots, count):
+def turn_in(piece, slots, count):
     order = lane_order()
 
     def body(turn, _):
-        for k in range(8):
-            t = turn * 8 + k
-            slots[t] = jnp.take_along_axis(source[t], order, axis=1).T
+        for k in range(16):
+            t = turn * 16 + k
+            slots[t] = jnp.take_along_axis(piece(t), order, axis=1).T
         return 0
 
-    lax.fori_loop(0, count // 8, body, 0)
-
-
-def vertical_kernel(source, charges, out, slots):
-    count = source.shape[0]
-    turn_in(source, slots, count)
-    zero = [jnp.zeros((SUB, SUB), jnp.float32) for _ in range(PARTS)]
-    walk(slots, slots, count, zero, charges, lambda t: t)
+    lax.fori_loop(0, count // 16, body, 0)
+
+
+def half_turn(value):
+    return pltpu.roll(value, SUB // 2, 0)
+
+
+def paths_kernel(
+    row_size,
+    col_size,
+    cost,
+    charges,
+    out_across,
+    out_down,
+    slots,
+    walked,
+    strips,
+    edge_out,
+    edge_in,
+    sent,
+    came,
+    back_out,
+    back_in,
+    edge_send,
+    edge_recv,
+    sent_sem,
+    came_sem,
+    back_send,
+    back_recv,
+):
+    count = out_across.shape[0]
+    height = strips.shape[0]
+    row = lax.axis_index("row")
+    me = lax.axis_index("col")
+    low = lax.broadcasted_iota(jnp.int32, (SUB, DISPARITIES), 0) < SUB // 2
     back = lane_order_back()
 
-    def body(turn, least):
-        for k in range(8):
-            t = turn * 8 + k
-            value = slots[t].T
-            out[t] = jnp.take_along_axis(value - least, back, axis=1)
-            least = jnp.min(value, axis=1, keepdims=True)
-        return least
-
-    lax.fori_loop(0, count // 8, body, jnp.zeros((SUB, 1), jnp.float32))
-
-
-def vertical_call(source, charges):
-    count = source.shape[0]
-    return pl.pallas_call(
-        vertical_kernel,
-        out_shape=jax.ShapeDtypeStruct(source.shape, jnp.float32),
-        in_specs=[
-            pl.BlockSpec(memory_space=pltpu.VMEM),
-            pl.BlockSpec(memory_space=pltpu.SMEM),
-        ],
-        out_specs=pl.BlockSpec(memory_space=pltpu.VMEM),
-        scratch_shapes=[pltpu.VMEM((count, DISPARITIES, SUB), jnp.float32)],
-        name="vertical_paths",
-    )(source, charges)
-
-
-def horizontal_kernel(
-    size, source, charges, out, slots, walked, edge_out, edge_in, send_sem, recv_sem
-):
-    count = source.shape[0]
-    me = lax.axis_index("col")
     barrier = pltpu.get_barrier_semaphore()
 
     @pl.when(me > 0)
     def _():
         pl.semaphore_signal(barrier, inc=1, device_id={"col": me - 1}, device_id_type=MESH)
 
-    @pl.when(me < size - 1)
+    @pl.when(me < col_size - 1)
     def _():
         pl.semaphore_signal(barrier, inc=1, device_id={"col": me + 1}, device_id_type=MESH)
 
-    neighbours = jnp.where(me > 0, 1, 0) + jnp.where(me < size - 1, 1, 0)
-    pl.semaphore_wait(barrier, neighbours)
-
-    turn_in(source, slots, count)
-    back = lane_order_back()
+    def greet(j, _):
+        peer = lax.rem(row + j, row_size)
+        pl.semaphore_signal(barrier, inc=1, device_id={"row": peer}, device_id_type=MESH)
+        return 0
+
+    lax.fori_loop(1, row_size, greet, 0)
+
+    def exchange(source, target, send_sem, recv_sem, what):
+        def copy(mine, slot):
+            return pltpu.make_async_remote_copy(
+                src_ref=source.at[mine],
+                dst_ref=target.at[slot],
+                send_sem=send_sem.at[mine],
+                recv_sem=recv_sem.at[slot],
+                device_id={"row": mine},
+                device_id_type=MESH,
+            )
+
+        def body(j, _):
+            peer = lax.rem(row + j, row_size)
+            if what == "start":
+                copy(peer, row).start()
+            elif what == "sent":
+                copy(peer, row).wait_send()
+            else:
+                copy(peer, peer).wait_recv()
+            return 0
+
+        lax.fori_loop(1, row_size, body, 0)
+        if what == "start":
+            target[row] = source[row]
+
+    def cut(tile, _):
+        start = pl.multiple_of(tile * SUB, SUB)
+        rows = [cost[y, pl.ds(start, SUB), :] for y in range(SUB)]
+        even = [jnp.where(low, rows[y], half_turn(rows[y + 1])) for y in range(0, SUB, 2)]
+        odd = [jnp.where(low, half_turn(rows[y]), rows[y + 1]) for y in range(0, SUB, 2)]
+        sent[2 * tile] = jnp.concatenate(even, axis=0).astype(jnp.bfloat16)
+        sent[2 * tile + 1] = jnp.concatenate(odd, axis=0).astype(jnp.bfloat16)
+        return 0
+
+    lax.fori_loop(0, row_size // 2, cut, 0)
+    neighbours = jnp.where(me > 0, 1, 0) + jnp.where(me < col_size - 1, 1, 0)
+    pl.semaphore_wait(barrier, neighbours + row_size - 1)
+    exchange(sent, came, sent_sem, came_sem, "start")
+    turn_in(lambda x: cost[:, x, :], slots, count)
+
+    def vertical_in():
+        exchange(sent, came, sent_sem, came_sem, "came")
+        order = lane_order()
+
+        def body(source, _):
+            near = came[source].astype(jnp.float32)
+            far = came[row_size - 1 - source].astype(jnp.float32)
+            for q in range(SUB // 2):
+                a = near[q * SUB : (q + 1) * SUB]
+                b = far[(3 - q) * SUB : (4 - q) * SUB]
+                first = jnp.where(low, a, b)
+                second = half_turn(jnp.where(low, b, a))
+                t = source * SUB + 2 * q
+                strips[t] = jnp.take_along_axis(first, order, axis=1).T
+                strips[t + 1] = jnp.take_along_axis(second, order, axis=1).T
+            return 0
+
+        lax.fori_loop(0, row_size, body, 0)
+
+    def vertical_walk():
+        zero = [jnp.zeros((SUB, SUB), jnp.float32) for _ in range(PARTS)]
+        walk(strips, strips, height, zero, charges, lambda t: t)
+
+    def vertical_out():
+        def layers(start):
+            before = strips[jnp.maximum(start - 1, 0)].T
+            least = jnp.min(before, axis=1, keepdims=True)
+            least = jnp.where(start == 0, 0.0, least)
+            found = []
+            for y in range(SUB):
+                value = strips[start + y].T
+                found.append(value - least)
+                least = jnp.min(value, axis=1, keepdims=True)
+            return found
+
+        def body(near, _):
+            far = row_size - 1 - near
+            one = layers(near * SUB)
+            other = layers(far * SUB)
+            total = [
+                jnp.take_along_axis(one[y] + half_turn(other[SUB - 1 - y]), back, axis=1)
+                for y in range(SUB)
+            ]
+            up = [jnp.where(low, total[y], half_turn(total[y + 1])) for y in (0, 2, 4, 6)]
+            down = [jnp.where(low, half_turn(total[y + 1]), total[y]) for y in (6, 4, 2, 0)]
+            back_out[near] = jnp.concatenate(up, axis=0).astype(jnp.bfloat16)
+            back_out[far] = jnp.concatenate(down, axis=0).astype(jnp.bfloat16)
+            return 0
+
+        lax.fori_loop(0, row_size // 2, body, 0)
+        exchange(back_out, back_in, back_send, back_recv, "start")
 
     def one_direction(way, first):
-        starts = me == (0 if way == 0 else size - 1)
-        ends = me == (size - 1 if way == 0 else 0)
+        starts = me == (0 if way == 0 else col_size - 1)
+        ends = me == (col_size - 1 if way == 0 else 0)
         toward = me + 1 if way == 0 else me - 1
         at = (lambda t: t) if way == 0 else (lambda t: count - 1 - t)
 
@@ -163,8 +252,8 @@
             return pltpu.make_async_remote_copy(
                 src_ref=edge_out.at[way],
                 dst_ref=edge_in.at[way],
-                send_sem=send_sem.at[way],
-                recv_sem=recv_sem.at[way],
+                send_sem=edge_send.at[way],
+                recv_sem=edge_recv.at[way],
                 device_id={"col": toward},
                 device_id_type=MESH,
             )
@@ -187,53 +276,91 @@
             copy().start()
 
         def body(turn, least):
-            for k in range(8):
-                t = at(turn * 8 + k)
+            for k in range(16):
+                t = at(turn * 16 + k)
                 value = walked[t].T
                 result = jnp.take_along_axis(value - least, back, axis=1)
-                out[t] = result if first else out[t] + result
+                out_across[t] = result if first else out_across[t] + result
                 least = jnp.min(value, axis=1, keepdims=True)
             return least
 
-        lax.fori_loop(0, count // 8, body, jnp.min(edge, axis=1, keepdims=True))
+        lax.fori_loop(0, count // 16, body, jnp.min(edge, axis=1, keepdims=True))
 
         @pl.when(jnp.logical_not(ends))
         def _():
             copy().wait_send()
 
-    @pl.when(me < size // 2)
+    place = jnp.minimum(me, col_size - 1 - me)
+    pieces = ((vertical_in, 3), (vertical_walk, 5), (vertical_out, 6))
+    for piece, threshold in pieces:
+        pl.when(place >= threshold)(piece)
+
+    @pl.when(me < col_size // 2)
     def _():
         one_direction(0, True)
+
+    @pl.when(me >= col_size // 2)
+    def _():
+        one_direction(1, True)
+
+    for piece, threshold in pieces:
+        pl.when(place < threshold)(piece)
+
+    @pl.when(me < col_size // 2)
+    def _():
         one_direction(1, False)
 
-    @pl.when(me >= size // 2)
-    def _():
-        one_direction(1, True)
+    @pl.when(me >= col_size // 2)
+    def _():
         one_direction(0, False)
 
-
-def horizontal_call(source, charges):
-    count = source.shape[0]
-    size = lax.axis_size("col")
+    exchange(back_out, back_in, back_send, back_recv, "came")
+
+    def hand_over(j, _):
+        out_down[j] = back_in[j]
+        return 0
+
+    lax.fori_loop(0, row_size, hand_over, 0)
+    exchange(sent, came, sent_sem, came_sem, "sent")
+    exchange(back_out, back_in, back_send, back_recv, "sent")
+
+
+def paths_call(cost, charges):
+    rows, count, _ = cost.shape
+    row_size, col_size = lax.axis_size("row"), lax.axis_size("col")
+    width = count // row_size
+    block = (row_size, rows * width, DISPARITIES)
+    vmem = pl.BlockSpec(memory_space=pltpu.VMEM)
     return pl.pallas_call(
-        functools.partial(horizontal_kernel, size),
-        out_shape=jax.ShapeDtypeStruct(source.shape, jnp.float32),
-        in_specs=[
-            pl.BlockSpec(memory_space=pltpu.VMEM),
-            pl.BlockSpec(memory_space=pltpu.SMEM),
-        ],
-        out_specs=pl.BlockSpec(memory_space=pltpu.VMEM),
+        functools.partial(paths_kernel, row_size, col_size),
+        out_shape=(
+            jax.ShapeDtypeStruct((count, rows, DISPARITIES), jnp.float32),
+            jax.ShapeDtypeStruct(block, jnp.bfloat16),
+        ),
+        in_specs=[vmem, pl.BlockSpec(memory_space=pltpu.SMEM)],
+        out_specs=(vmem, vmem),
         scratch_shapes=[
             pltpu.VMEM((count, DISPARITIES, SUB), jnp.float32),
             pltpu.VMEM((count, DISPARITIES, SUB), jnp.float32),
+            pltpu.VMEM((rows * row_size, DISPARITIES, SUB), jnp.float32),
             pltpu.VMEM((2, SUB, DISPARITIES), jnp.float32),
             pltpu.VMEM((2, SUB, DISPARITIES), jnp.float32),
+            pltpu.VMEM(block, jnp.bfloat16),
+            pltpu.VMEM(block, jnp.bfloat16),
+            pltpu.VMEM(block, jnp.bfloat16),
+            pltpu.VMEM(block, jnp.bfloat16),
             pltpu.SemaphoreType.DMA((2,)),
             pltpu.SemaphoreType.DMA((2,)),
+            pltpu.SemaphoreType.DMA((row_size,)),
+            pltpu.SemaphoreType.DMA((row_size,)),
+            pltpu.SemaphoreType.DMA((row_size,)),
+            pltpu.SemaphoreType.DMA((row_size,)),
         ],
-        compiler_params=pltpu.CompilerParams(collective_id=0, has_side_effects=True),
-        name="horizontal_paths",
-    )(source, charges)
+        compiler_params=pltpu.CompilerParams(
+            collective_id=0, has_side_effects=True, vmem_limit_bytes=60 * 1024 * 1024
+        ),
+        name="four_paths",
+    )(cost, charges)
 
 
 def conv_stack(stereo_neuron_outputs, filter_tap_coefficients, filter_stack_intercepts):
@@ -303,15 +430,10 @@
     skewed = flat.reshape(rows_here, cols_here, cols_here + DISPARITIES + 1)[:, :, :DISPARITIES]
     similarity = skewed[:, :, ::-1]
     cost = jnp.where(reference_picture_present[:, :, None] == 1, 1.0 - similarity, 1.0)
-    horizontal = horizontal_call(jnp.swapaxes(cost, 0, 1), smoothness_charges)
-    strip = lax.all_to_all(
-        cost.astype(jnp.bfloat16), "row", split_axis=1, concat_axis=0, tiled=True
-    ).astype(jnp.float32)
-    width = strip.shape[1]
-    both = vertical_call(jnp.concatenate([strip, strip[::-1]], axis=1), smoothness_charges)
-    vertical = (both[:, :width] + both[::-1, width:]).astype(jnp.bfloat16)
-    vertical = lax.all_to_all(vertical, "row", split_axis=0, concat_axis=1, tiled=True)
-    return vertical.astype(jnp.float32) + jnp.swapaxes(horizontal, 0, 1)
+    across, down = paths_call(cost, smoothness_charges)
+    down = down.reshape(lax.axis_size("row"), rows_here, -1, DISPARITIES).astype(jnp.float32)
+    down = jnp.swapaxes(down, 0, 1).reshape(cost.shape)
+    return down + jnp.swapaxes(across, 0, 1)
 
 
 def solution(mesh):

time: 226 us -> 168 us (0.74)
  the two profiles are of different devices: /device:TPU:2 before, /device:TPU:32 now
where the time goes in v2:
time: 168 us
  Pallas kernels  116 us (69%)
  starting transfers between devices  23.8 us (14%)
  matrix products  10.6 us (6%)
  waiting for transfers between devices  6.98 us (4%)
  local copies, waits for them, and re-layouts  5.96 us (4%)
  other arithmetic  2.93 us (2%)
    pallas_call x1, Pallas kernels, paths_call(): pl.pallas_call(functools.partial(paths_kernel, row_size, col_size), out_s...  116 us
    ppermute x3, starting transfers between devices, from_behind(): return lax.ppermute(block, axis, route)  14.4 us
    dot_general x27, matrix products, conv_stack(): jnp.einsum('oc,iycx->iyox', filter_tap_coefficients[layer_number, tap_row...  10.1 us
    ppermute x2, waiting for transfers between devices, extended_2(): after = lax.ppermute(first, axis, down)  5.02 us
    ppermute x2, starting transfers between devices, extended_2(): before = lax.ppermute(last, axis, up)  4.85 us
    ppermute x2, starting transfers between devices, extended_2(): after = lax.ppermute(first, axis, down)  4.63 us
  transfers between devices with their start and end apart: 7, of which 4 were waited for; matrix products, arithmetic and copies ran while one was open for 1% of the time, Pallas kernels for 0%

profile of v2, /device:TPU:32, one launch (start us, length us, event | category | flops | bytes accessed | tf_op | source)
XLA Modules:
  0.0 167.5 jit_solution(1392166988546066698)
XLA Ops:
  0.0 1.0 fusion.112
  1.0 3.4 %collective-permute-start = (bf16[2,3,64,128]{3,2,1,0:T(8,128)(2,1)S(1)}, bf16[2,3,64,128]{3,2,1,0:T(8,128)(2,1)S(1)}, u32[]{:S(2)}, u32[]{:S(2)}) collective-permute-start(bf16[2,3,64,128]{3,2,1,0:T(8,128)(2,1)S(1)} %get-tuple-element.12), channel_id=1, source_target_pairs={{0,16},{16,32},{32,48},{48,64},{64,80},{80,96},{96,112},{112,128},... | collective-permute-start | bytes 294920 | tf_op jit(solution)/shard_map/ppermute | solution.py:29
  4.4 3.3 %collective-permute-start.1 = (bf16[2,3,64,128]{3,2,1,0:T(8,128)(2,1)S(1)}, bf16[2,3,64,128]{3,2,1,0:T(8,128)(2,1)S(1)}, u32[]{:S(2)}, u32[]{:S(2)}) collective-permute-start(bf16[2,3,64,128]{3,2,1,0:T(8,128)(2,1)S(1)} %get-tuple-element.11), channel_id=1, source_target_pairs={{16,0},{32,16},{48,32},{64,48},{80,64},{96,80},{112,96},{128,112},... | collective-permute-start | bytes 294920 | tf_op jit(solution)/shard_map/ppermute | solution.py:30
  7.8 0.1 broadcast_and_fusion
  7.9 0.1 broadcast_and_fusion.1
  7.9 0.4 collective-permute-done
  8.4 1.0 constant_dynamic-update-slice_fusion.1
  9.4 1.5 collective-permute-done.1
  10.9 0.2 fusion.111
  11.1 0.0 copy-start.1
  11.2 1.4 collective-permute-start.2
  12.6 1.3 collective-permute-start.3
  13.9 0.0 copy-done.3
  14.6 0.0 collective-permute-done.2
  14.6 3.5 %collective-permute-done.3 = bf16[2,14,64,3]{3,2,1,0:T(8,128)(2,1)S(1)} collective-permute-done((bf16[2,14,64,3]{3,2,1,0:T(8,128)(2,1)S(1)}, bf16[2,14,64,3]{3,2,1,0:T(8,128)(2,1)S(1)}, u32[]{:S(2)}, u32[]{:S(2)}) %collective-permute-start.3) | collective-permute-done | bytes 10784 | tf_op jit(solution)/shard_map/ppermute | solution.py:30
  18.1 0.6 pad_maximum_fusion
  18.7 0.0 copy-done.1
  18.7 0.4 fusion.13
  19.1 0.3 fusion.15
  19.5 0.4 fusion.17
  19.9 0.4 fusion.19
  20.3 0.3 fusion.21
  20.7 0.4 fusion.23
  21.1 0.4 fusion.25
  21.5 0.3 fusion.27
  21.9 1.1 fusion.10
  23.0 0.3 fusion.37
  23.4 0.4 convolution_add_fusion.7
  23.8 0.4 convolution_add_fusion.6
  24.2 0.3 convolution_add_fusion.5
  24.5 0.4 convolution_add_fusion.4
  24.9 0.4 convolution_add_fusion.3
  25.3 0.3 convolution_add_fusion.2
  25.6 0.4 convolution_add_fusion.1
  26.0 0.4 fusion.4
  26.5 0.2 fusion.53
  26.7 0.3 convolution_add_fusion.15
  27.0 0.3 convolution_add_fusion.14
  27.3 0.2 convolution_add_fusion.13
  27.5 0.3 convolution_add_fusion.12
  27.8 0.3 convolution_add_fusion.11
  28.1 0.2 convolution_add_fusion.10
  28.3 0.0 copy-start.2
  28.3 0.3 convolution_add_fusion.9
  28.6 0.3 multiply_reduce_fusion
  29.0 0.1 fusion.39
  29.0 9.7 %collective-permute-start.4 = (bf16[8,64,128]{2,1,0:T(8,128)(2,1)S(1)}, bf16[8,64,128]{2,1,0:T(8,128)(2,1)S(1)}, u32[]{:S(2)}, u32[]{:S(2)}) collective-permute-start(bf16[8,64,128]{2,1,0:T(8,128)(2,1)S(1)} %slice_bitcast_fusion), channel_id=1, source_target_pairs={{0,3},{1,4},{2,5},{3,6},{4,7},{5,8},{6,9},{7,10},{8,11},{9,12},{10... | collective-permute-start | bytes 393224 | tf_op jit(solution)/shard_map/ppermute | solution.py:19
  38.7 3.2 %collective-permute-start.5 = (bf16[8,64,128]{2,1,0:T(8,128)(2,1)S(1)}, bf16[8,64,128]{2,1,0:T(8,128)(2,1)S(1)}, u32[]{:S(2)}, u32[]{:S(2)}) collective-permute-start(bf16[8,64,128]{2,1,0:T(8,128)(2,1)S(1)} %slice_bitcast_fusion), channel_id=1, source_target_pairs={{0,2},{1,3},{2,4},{3,5},{4,6},{5,7},{6,8},{7,9},{8,10},{9,11},{10,... | collective-permute-start | bytes 393224 | tf_op jit(solution)/shard_map/ppermute | solution.py:19
  41.9 1.5 collective-permute-start.6
  43.5 0.0 collective-permute-done.4
  43.5 1.5 collective-permute-done.5
  45.0 0.0 collective-permute-done.6
  45.0 0.6 fusion.43
  45.6 0.1 pad_bitcast_fusion
  45.7 0.6 copy.38
  46.3 0.1 pad.9
  46.4 1.3 reshape.125
  47.7 0.7 rev.3
  48.4 1.0 subtract_select_fusion.cost
  49.4 116.0 %four_paths.1 = (f32[128,8,128]{2,1,0:T(8,128)}, bf16[32,32,128]{2,1,0:T(8,128)(2,1)}) custom-call(f32[8,128,128]{2,1,0:T(8,128)} %subtract_select_fusion.cost, s32[2]{0:T(128)} %charges.1), custom_call_target="tpu_custom_call" | custom-call | tf_op jit(solution)/shard_map/four_paths/pallas_call | solution.py:334
  165.4 1.1 convert.6
  166.5 0.0 copy-done
  166.6 0.1 bitcast_add_fusion
  166.6 0.9 copy.10
  (15 shorter events, 0.2 us)
Async XLA Ops:
  0.0 13.9 %copy-start.3 = (f32[3,64]{1,0:T(4,128)S(1)}, f32[3,64]{1,0:T(4,128)}, u32[]{:S(2)}) copy-start(f32[3,64]{1,0:T(4,128)} %param.8) | copy-start | bytes 2308
  1.0 7.4 %collective-permute-start = (bf16[2,3,64,128]{3,2,1,0:T(8,128)(2,1)S(1)}, bf16[2,3,64,128]{3,2,1,0:T(8,128)(2,1)S(1)}, u32[]{:S(2)}, u32[]{:S(2)}) collective-permute-start(bf16[2,3,64,128]{3,2,1,0:T(8,128)(2,1)S(1)} %get-tuple-element.12), channel_id=1, source_target_pairs={{0,16},{16,32},{32,48},{48,64},{64,80},{80,96},{96,112},{112,128},... | collective-permute-start | bytes 294920 | tf_op jit(solution)/shard_map/ppermute | solution.py:29
  4.4 6.5 %collective-permute-start.1 = (bf16[2,3,64,128]{3,2,1,0:T(8,128)(2,1)S(1)}, bf16[2,3,64,128]{3,2,1,0:T(8,128)(2,1)S(1)}, u32[]{:S(2)}, u32[]{:S(2)}) collective-permute-start(bf16[2,3,64,128]{3,2,1,0:T(8,128)(2,1)S(1)} %get-tuple-element.11), channel_id=1, source_target_pairs={{16,0},{32,16},{48,32},{64,48},{80,64},{96,80},{112,96},{128,112},... | collective-permute-start | bytes 294920 | tf_op jit(solution)/shard_map/ppermute | solution.py:30
  11.1 7.5 %copy-start.1 = (bf16[3,3,3,64,64]{4,3,2,1,0:T(8,128)(2,1)S(1)}, bf16[3,3,3,64,64]{4,3,2,1,0:T(8,128)(2,1)}, u32[]{:S(2)}) copy-start(bf16[3,3,3,64,64]{4,3,2,1,0:T(8,128)(2,1)} %param.7) | copy-start | bytes 663556
  11.2 3.4 %collective-permute-start.2 = (bf16[2,14,64,3]{3,2,1,0:T(8,128)(2,1)S(1)}, bf16[2,14,64,3]{3,2,1,0:T(8,128)(2,1)S(1)}, u32[]{:S(2)}, u32[]{:S(2)}) collective-permute-start(bf16[2,14,64,3]{3,2,1,0:T(8,128)(2,1)S(1)} %get-tuple-element.9), channel_id=1, source_target_pairs={{0,1},{1,2},{2,3},{3,4},{4,5},{5,6},{6,7},{7,8},{8,9},{9,10},{10,1... | collective-permute-start | bytes 32264 | tf_op jit(solution)/shard_map/ppermute | solution.py:29
  12.6 5.5 %collective-permute-start.3 = (bf16[2,14,64,3]{3,2,1,0:T(8,128)(2,1)S(1)}, bf16[2,14,64,3]{3,2,1,0:T(8,128)(2,1)S(1)}, u32[]{:S(2)}, u32[]{:S(2)}) collective-permute-start(bf16[2,14,64,3]{3,2,1,0:T(8,128)(2,1)S(1)} %get-tuple-element.10), channel_id=1, source_target_pairs={{1,0},{2,1},{3,2},{4,3},{5,4},{6,5},{7,6},{8,7},{9,8},{10,9},{11,1... | collective-permute-start | bytes 32264 | tf_op jit(solution)/shard_map/ppermute | solution.py:30
  28.3 15.1 %copy-start.2 = (s32[8,128]{1,0:T(8,128)S(1)}, s32[8,128]{1,0:T(8,128)}, u32[]{:S(2)}) copy-start(s32[8,128]{1,0:T(8,128)} %param.9) | copy-start | bytes 12292
  29.0 14.4 %collective-permute-start.4 = (bf16[8,64,128]{2,1,0:T(8,128)(2,1)S(1)}, bf16[8,64,128]{2,1,0:T(8,128)(2,1)S(1)}, u32[]{:S(2)}, u32[]{:S(2)}) collective-permute-start(bf16[8,64,128]{2,1,0:T(8,128)(2,1)S(1)} %slice_bitcast_fusion), channel_id=1, source_target_pairs={{0,3},{1,4},{2,5},{3,6},{4,7},{5,8},{6,9},{7,10},{8,11},{9,12},{10... | collective-permute-start | bytes 393224 | tf_op jit(solution)/shard_map/ppermute | solution.py:19
  38.7 6.2 %collective-permute-start.5 = (bf16[8,64,128]{2,1,0:T(8,128)(2,1)S(1)}, bf16[8,64,128]{2,1,0:T(8,128)(2,1)S(1)}, u32[]{:S(2)}, u32[]{:S(2)}) collective-permute-start(bf16[8,64,128]{2,1,0:T(8,128)(2,1)S(1)} %slice_bitcast_fusion), channel_id=1, source_target_pairs={{0,2},{1,3},{2,4},{3,5},{4,6},{5,7},{6,8},{7,9},{8,10},{9,11},{10,... | collective-permute-start | bytes 393224 | tf_op jit(solution)/shard_map/ppermute | solution.py:19
  41.9 3.0 %collective-permute-start.6 = (bf16[8,64,128]{2,1,0:T(8,128)(2,1)S(1)}, bf16[8,64,128]{2,1,0:T(8,128)(2,1)S(1)}, u32[]{:S(2)}, u32[]{:S(2)}) collective-permute-start(bf16[8,64,128]{2,1,0:T(8,128)(2,1)S(1)} %slice_bitcast_fusion), channel_id=1, source_target_pairs={{0,1},{1,2},{2,3},{3,4},{4,5},{5,6},{6,7},{7,8},{8,9},{9,10},{10,1... | collective-permute-start | bytes 393224 | tf_op jit(solution)/shard_map/ppermute | solution.py:19
  165.4 1.1 copy-start

commit v3 on v2

--- a/solution.py
+++ b/solution.py
@@ -32,14 +32,23 @@
     return value
 
 
-def lane_order():
-    lane = lax.broadcasted_iota(jnp.int32, (SUB, DISPARITIES), 1)
-    return (lane % SUB) * PARTS + lane // SUB
-
-
-def lane_order_back():
-    lane = lax.broadcasted_iota(jnp.int32, (SUB, DISPARITIES), 1)
-    return (lane % PARTS) * SUB + lane // PARTS
+def order_matrix():
+    row = lax.broadcasted_iota(jnp.int32, (DISPARITIES, DISPARITIES), 0)
+    lane = lax.broadcasted_iota(jnp.int32, (DISPARITIES, DISPARITIES), 1)
+    return jnp.where(lane == (row % SUB) * PARTS + row // SUB, 1.0, 0.0).astype(jnp.bfloat16)
+
+
+def turned(value, order):
+    return lax.dot_general(
+        order,
+        value.astype(jnp.bfloat16),
+        (((1,), (1,)), ((), ())),
+        preferred_element_type=jnp.float32,
+    )
+
+
+def ordered(value, order):
+    return jnp.dot(value, order, preferred_element_type=jnp.float32)
 
 
 def pieces_of(value):
@@ -61,39 +70,46 @@
     below = jnp.where(first_sub, jnp.inf, pltpu.roll(lifted[-1], 1, 0))
     above = jnp.where(last_sub, jnp.inf, pltpu.roll(lifted[0], SUB - 1, 0))
     near = [below] + lifted + [above]
-    jump = smallest(state) + p2
-    return [
+    least = smallest(state)
+    jump = least + p2
+    fresh = [
         cost[v]
         + jnp.minimum(jnp.minimum(state[v], jnp.minimum(near[v], near[v + 2])), jump)
         for v in range(PARTS)
     ]
-
-
-def walk(slots, out, count, state, charges, at):
+    return fresh, least
+
+
+def walk(slots, out, leasts, count, state, charges, at):
     sub = lax.broadcasted_iota(jnp.int32, (SUB, SUB), 0)
     first_sub, last_sub = sub == 0, sub == SUB - 1
     p1 = charges[0].astype(jnp.float32) / 64.0
     p2 = charges[1].astype(jnp.float32) / 64.0
 
-    def body(turn, state):
-        state = list(state)
+    def body(turn, carry):
+        state, least = list(carry[0]), carry[1]
         for k in range(8):
             t = at(turn * 8 + k)
-            state = step_once(state, pieces_of(slots[t]), p1, p2, first_sub, last_sub)
+            state, least = step_once(state, pieces_of(slots[t]), p1, p2, first_sub, last_sub)
+            leasts[t] = least
             for v in range(PARTS):
                 out[t, v * SUB : (v + 1) * SUB, :] = state[v]
-        return tuple(state)
-
-    return list(lax.fori_loop(0, count // 8, body, tuple(state)))
-
-
-def turn_in(piece, slots, count):
-    order = lane_order()
-
+        return tuple(state), least
+
+    start = (tuple(state), jnp.zeros((SUB, SUB), jnp.float32))
+    return lax.fori_loop(0, count // 8, body, start)
+
+
+def layer(walked, leasts, t):
+    least = leasts[t]
+    return jnp.concatenate([piece - least for piece in pieces_of(walked[t])], axis=0).T
+
+
+def turn_in(piece, slots, count, order):
     def body(turn, _):
         for k in range(16):
             t = turn * 16 + k
-            slots[t] = jnp.take_along_axis(piece(t), order, axis=1).T
+            slots[t] = turned(piece(t), order)
         return 0
 
     lax.fori_loop(0, count // 16, body, 0)
@@ -113,6 +129,8 @@
     slots,
     walked,
     strips,
+    leasts,
+    strip_leasts,
     edge_out,
     edge_in,
     sent,
@@ -131,7 +149,7 @@
     row = lax.axis_index("row")
     me = lax.axis_index("col")
     low = lax.broadcasted_iota(jnp.int32, (SUB, DISPARITIES), 0) < SUB // 2
-    back = lane_order_back()
+    order = order_matrix()
 
     barrier = pltpu.get_barrier_semaphore()
 
@@ -188,11 +206,10 @@
     neighbours = jnp.where(me > 0, 1, 0) + jnp.where(me < col_size - 1, 1, 0)
     pl.semaphore_wait(barrier, neighbours + row_size - 1)
     exchange(sent, came, sent_sem, came_sem, "start")
-    turn_in(lambda x: cost[:, x, :], slots, count)
+    turn_in(lambda x: cost[:, x, :], slots, count, order)
 
     def vertical_in():
         exchange(sent, came, sent_sem, came_sem, "came")
-        order = lane_order()
 
         def body(source, _):
             near = came[source].astype(jnp.float32)
@@ -203,40 +220,29 @@
                 first = jnp.where(low, a, b)
                 second = half_turn(jnp.where(low, b, a))
                 t = source * SUB + 2 * q
-                strips[t] = jnp.take_along_axis(first, order, axis=1).T
-                strips[t + 1] = jnp.take_along_axis(second, order, axis=1).T
+                strips[t] = turned(first, order)
+                strips[t + 1] = turned(second, order)
             return 0
 
         lax.fori_loop(0, row_size, body, 0)
 
     def vertical_walk():
         zero = [jnp.zeros((SUB, SUB), jnp.float32) for _ in range(PARTS)]
-        walk(strips, strips, height, zero, charges, lambda t: t)
+        walk(strips, strips, strip_leasts, height, zero, charges, lambda t: t)
 
     def vertical_out():
-        def layers(start):
-            before = strips[jnp.maximum(start - 1, 0)].T
-            least = jnp.min(before, axis=1, keepdims=True)
-            least = jnp.where(start == 0, 0.0, least)
-            found = []
-            for y in range(SUB):
-                value = strips[start + y].T
-                found.append(value - least)
-                least = jnp.min(value, axis=1, keepdims=True)
-            return found
-
         def body(near, _):
             far = row_size - 1 - near
-            one = layers(near * SUB)
-            other = layers(far * SUB)
-            total = [
-                jnp.take_along_axis(one[y] + half_turn(other[SUB - 1 - y]), back, axis=1)
-                for y in range(SUB)
-            ]
+            one = [layer(strips, strip_leasts, near * SUB + y) for y in range(SUB)]
+            other = [layer(strips, strip_leasts, far * SUB + y) for y in range(SUB)]
+            total = [one[y] + half_turn(other[SUB - 1 - y]) for y in range(SUB)]
             up = [jnp.where(low, total[y], half_turn(total[y + 1])) for y in (0, 2, 4, 6)]
             down = [jnp.where(low, half_turn(total[y + 1]), total[y]) for y in (6, 4, 2, 0)]
-            back_out[near] = jnp.concatenate(up, axis=0).astype(jnp.bfloat16)
-            back_out[far] = jnp.concatenate(down, axis=0).astype(jnp.bfloat16)
+            both = jnp.concatenate(up + down, axis=0).astype(jnp.bfloat16)
+            both = ordered(both, order).astype(jnp.bfloat16)
+            half = SUB * SUB // 2
+            back_out[near] = both[:half]
+            back_out[far] = both[half:]
             return 0
 
         lax.fori_loop(0, row_size // 2, body, 0)
@@ -260,31 +266,38 @@
 
         @pl.when(starts)
         def _():
-            edge_in[way] = jnp.zeros((SUB, DISPARITIES), jnp.float32)
+            edge_in[way] = jnp.zeros((DISPARITIES, SUB), jnp.float32)
 
         @pl.when(jnp.logical_not(starts))
         def _():
             copy().wait_recv()
 
-        edge = edge_in[way]
-        state = walk(slots, walked, count, pieces_of(edge.T), charges, at)
-        last = jnp.concatenate(state, axis=0).T
+        state, least = walk(
+            slots, walked, leasts, count, pieces_of(edge_in[way]), charges, at
+        )
 
         @pl.when(jnp.logical_not(ends))
         def _():
-            edge_out[way] = last - jnp.min(last, axis=1, keepdims=True)
+            edge_out[way] = jnp.concatenate([piece - least for piece in state], axis=0)
             copy().start()
 
-        def body(turn, least):
-            for k in range(16):
-                t = at(turn * 16 + k)
-                value = walked[t].T
-                result = jnp.take_along_axis(value - least, back, axis=1)
-                out_across[t] = result if first else out_across[t] + result
-                least = jnp.min(value, axis=1, keepdims=True)
-            return least
-
-        lax.fori_loop(0, count // 16, body, jnp.min(edge, axis=1, keepdims=True))
+        def body(turn, _):
+            start = turn * 16
+            results = [layer(walked, leasts, start + k) for k in range(16)]
+            if first:
+                for k in range(16):
+                    out_across[start + k] = results[k]
+            else:
+                total = [out_across[start + k] + results[k] for k in range(16)]
+                total = jnp.concatenate(total, axis=0)
+                high = total.astype(jnp.bfloat16)
+                rest = (total - high.astype(jnp.float32)).astype(jnp.bfloat16)
+                total = ordered(high, order) + ordered(rest, order)
+                for k in range(16):
+                    out_across[start + k] = total[k * SUB : (k + 1) * SUB]
+            return 0
+
+        lax.fori_loop(0, count // 16, body, 0)
 
         @pl.when(jnp.logical_not(ends))
         def _():
@@ -343,8 +356,10 @@
             pltpu.VMEM((count, DISPARITIES, SUB), jnp.float32),
             pltpu.VMEM((count, DISPARITIES, SUB), jnp.float32),
             pltpu.VMEM((rows * row_size, DISPARITIES, SUB), jnp.float32),
-            pltpu.VMEM((2, SUB, DISPARITIES), jnp.float32),
-            pltpu.VMEM((2, SUB, DISPARITIES), jnp.float32),
+            pltpu.VMEM((count, SUB, SUB), jnp.float32),
+            pltpu.VMEM((rows * row_size, SUB, SUB), jnp.float32),
+            pltpu.VMEM((2, DISPARITIES, SUB), jnp.float32),
+            pltpu.VMEM((2, DISPARITIES, SUB), jnp.float32),
             pltpu.VMEM(block, jnp.bfloat16),
             pltpu.VMEM(block, jnp.bfloat16),
             pltpu.VMEM(block, jnp.bfloat16),

time: 168 us -> 155 us (0.923)
  the two profiles are of different devices: /device:TPU:32 before, /device:TPU:66 now
where the time goes in v3:
time: 155 us
  Pallas kernels  102 us (66%)
  starting transfers between devices  22.9 us (15%)
  matrix products  10.7 us (7%)
  waiting for transfers between devices  9.19 us (6%)
  local copies, waits for them, and re-layouts  5.96 us (4%)
  other arithmetic  2.93 us (2%)
    pallas_call x1, Pallas kernels, paths_call(): pl.pallas_call(functools.partial(paths_kernel, row_size, col_size), out_s...  102 us
    ppermute x3, starting transfers between devices, from_behind(): return lax.ppermute(block, axis, route)  14.4 us
    dot_general x27, matrix products, conv_stack(): jnp.einsum('oc,iycx->iyox', filter_tap_coefficients[layer_number, tap_row...  10.1 us
    ppermute x2, waiting for transfers between devices, extended_2(): after = lax.ppermute(first, axis, down)  7.21 us
    ppermute x2, starting transfers between devices, extended_2(): before = lax.ppermute(last, axis, up)  5.25 us
    ppermute x2, starting transfers between devices, extended_2(): after = lax.ppermute(first, axis, down)  3.34 us
  transfers between devices with their start and end apart: 7, of which 4 were waited for; matrix products, arithmetic and copies ran while one was open for 1% of the time, Pallas kernels for 0%

profile of v3, /device:TPU:66, one launch (start us, length us, event | category | flops | bytes accessed | tf_op | source)
XLA Modules:
  0.0 154.5 jit_solution(5960721596402344086)
XLA Ops:
  0.0 1.0 fusion.112
  1.0 3.8 %collective-permute-start = (bf16[2,3,64,128]{3,2,1,0:T(8,128)(2,1)S(1)}, bf16[2,3,64,128]{3,2,1,0:T(8,128)(2,1)S(1)}, u32[]{:S(2)}, u32[]{:S(2)}) collective-permute-start(bf16[2,3,64,128]{3,2,1,0:T(8,128)(2,1)S(1)} %get-tuple-element.12), channel_id=1, source_target_pairs={{0,16},{16,32},{32,48},{48,64},{64,80},{80,96},{96,112},{112,128},... | collective-permute-start | bytes 294920 | tf_op jit(solution)/shard_map/ppermute | solution.py:29
  4.8 2.0 %collective-permute-start.1 = (bf16[2,3,64,128]{3,2,1,0:T(8,128)(2,1)S(1)}, bf16[2,3,64,128]{3,2,1,0:T(8,128)(2,1)S(1)}, u32[]{:S(2)}, u32[]{:S(2)}) collective-permute-start(bf16[2,3,64,128]{3,2,1,0:T(8,128)(2,1)S(1)} %get-tuple-element.11), channel_id=1, source_target_pairs={{16,0},{32,16},{48,32},{64,48},{80,64},{96,80},{112,96},{128,112},... | collective-permute-start | bytes 294920 | tf_op jit(solution)/shard_map/ppermute | solution.py:30
  6.9 0.1 broadcast_and_fusion
  7.0 0.1 broadcast_and_fusion.1
  7.0 0.4 collective-permute-done
  7.5 1.0 constant_dynamic-update-slice_fusion.1
  8.5 3.7 %collective-permute-done.1 = bf16[2,3,64,128]{3,2,1,0:T(8,128)(2,1)S(1)} collective-permute-done((bf16[2,3,64,128]{3,2,1,0:T(8,128)(2,1)S(1)}, bf16[2,3,64,128]{3,2,1,0:T(8,128)(2,1)S(1)}, u32[]{:S(2)}, u32[]{:S(2)}) %collective-permute-start.1) | collective-permute-done | bytes 98336 | tf_op jit(solution)/shard_map/ppermute | solution.py:30
  12.2 0.2 fusion.111
  12.4 0.0 copy-start.1
  12.5 1.4 collective-permute-start.2
  13.9 1.3 collective-permute-start.3
  15.2 0.0 copy-done.3
  15.9 0.0 collective-permute-done.2
  15.9 3.5 %collective-permute-done.3 = bf16[2,14,64,3]{3,2,1,0:T(8,128)(2,1)S(1)} collective-permute-done((bf16[2,14,64,3]{3,2,1,0:T(8,128)(2,1)S(1)}, bf16[2,14,64,3]{3,2,1,0:T(8,128)(2,1)S(1)}, u32[]{:S(2)}, u32[]{:S(2)}) %collective-permute-start.3) | collective-permute-done | bytes 10784 | tf_op jit(solution)/shard_map/ppermute | solution.py:30
  19.4 0.6 pad_maximum_fusion
  20.0 0.0 copy-done.1
  20.0 0.4 fusion.13
  20.4 0.3 fusion.15
  20.8 0.4 fusion.17
  21.2 0.4 fusion.19
  21.6 0.3 fusion.21
  22.0 0.4 fusion.23
  22.4 0.4 fusion.25
  22.9 0.3 fusion.27
  23.2 1.1 fusion.10
  24.4 0.3 fusion.37
  24.7 0.4 convolution_add_fusion.7
  25.1 0.4 convolution_add_fusion.6
  25.5 0.3 convolution_add_fusion.5
  25.8 0.4 convolution_add_fusion.4
  26.2 0.4 convolution_add_fusion.3
  26.6 0.3 convolution_add_fusion.2
  27.0 0.4 convolution_add_fusion.1
  27.4 0.4 fusion.4
  27.8 0.2 fusion.53
  28.0 0.3 convolution_add_fusion.15
  28.3 0.3 convolution_add_fusion.14
  28.6 0.2 convolution_add_fusion.13
  28.8 0.3 convolution_add_fusion.12
  29.1 0.3 convolution_add_fusion.11
  29.4 0.2 convolution_add_fusion.10
  29.6 0.0 copy-start.2
  29.7 0.3 convolution_add_fusion.9
  30.0 0.3 multiply_reduce_fusion
  30.3 0.1 fusion.39
  30.4 9.7 %collective-permute-start.4 = (bf16[8,64,128]{2,1,0:T(8,128)(2,1)S(1)}, bf16[8,64,128]{2,1,0:T(8,128)(2,1)S(1)}, u32[]{:S(2)}, u32[]{:S(2)}) collective-permute-start(bf16[8,64,128]{2,1,0:T(8,128)(2,1)S(1)} %slice_bitcast_fusion), channel_id=1, source_target_pairs={{0,3},{1,4},{2,5},{3,6},{4,7},{5,8},{6,9},{7,10},{8,11},{9,12},{10... | collective-permute-start | bytes 393224 | tf_op jit(solution)/shard_map/ppermute | solution.py:19
  40.1 3.2 %collective-permute-start.5 = (bf16[8,64,128]{2,1,0:T(8,128)(2,1)S(1)}, bf16[8,64,128]{2,1,0:T(8,128)(2,1)S(1)}, u32[]{:S(2)}, u32[]{:S(2)}) collective-permute-start(bf16[8,64,128]{2,1,0:T(8,128)(2,1)S(1)} %slice_bitcast_fusion), channel_id=1, source_target_pairs={{0,2},{1,3},{2,4},{3,5},{4,6},{5,7},{6,8},{7,9},{8,10},{9,11},{10,... | collective-permute-start | bytes 393224 | tf_op jit(solution)/shard_map/ppermute | solution.py:19
  43.3 1.5 collective-permute-start.6
  44.8 0.0 collective-permute-done.4
  44.8 1.5 collective-permute-done.5
  46.3 0.0 collective-permute-done.6
  46.3 0.6 fusion.43
  46.9 0.1 pad_bitcast_fusion
  47.0 0.6 copy.38
  47.6 0.1 pad.9
  47.7 1.3 reshape.125
  49.0 0.7 rev.3
  49.8 1.0 subtract_select_fusion.cost
  50.8 101.7 %four_paths.1 = (f32[128,8,128]{2,1,0:T(8,128)}, bf16[32,32,128]{2,1,0:T(8,128)(2,1)}) custom-call(f32[8,128,128]{2,1,0:T(8,128)} %subtract_select_fusion.cost, s32[2]{0:T(128)} %charges.1), custom_call_target="tpu_custom_call" | custom-call | tf_op jit(solution)/shard_map/four_paths/pallas_call | solution.py:347
  152.5 1.1 convert.6
  153.6 0.0 copy-done
  153.6 0.1 bitcast_add_fusion
  153.6 0.9 copy.10
  (15 shorter events, 0.2 us)
Async XLA Ops:
  0.0 15.2 %copy-start.3 = (f32[3,64]{1,0:T(4,128)S(1)}, f32[3,64]{1,0:T(4,128)}, u32[]{:S(2)}) copy-start(f32[3,64]{1,0:T(4,128)} %param.8) | copy-start | bytes 2308
  1.0 6.5 %collective-permute-start = (bf16[2,3,64,128]{3,2,1,0:T(8,128)(2,1)S(1)}, bf16[2,3,64,128]{3,2,1,0:T(8,128)(2,1)S(1)}, u32[]{:S(2)}, u32[]{:S(2)}) collective-permute-start(bf16[2,3,64,128]{3,2,1,0:T(8,128)(2,1)S(1)} %get-tuple-element.12), channel_id=1, source_target_pairs={{0,16},{16,32},{32,48},{48,64},{64,80},{80,96},{96,112},{112,128},... | collective-permute-start | bytes 294920 | tf_op jit(solution)/shard_map/ppermute | solution.py:29
  4.8 7.4 %collective-permute-start.1 = (bf16[2,3,64,128]{3,2,1,0:T(8,128)(2,1)S(1)}, bf16[2,3,64,128]{3,2,1,0:T(8,128)(2,1)S(1)}, u32[]{:S(2)}, u32[]{:S(2)}) collective-permute-start(bf16[2,3,64,128]{3,2,1,0:T(8,128)(2,1)S(1)} %get-tuple-element.11), channel_id=1, source_target_pairs={{16,0},{32,16},{48,32},{64,48},{80,64},{96,80},{112,96},{128,112},... | collective-permute-start | bytes 294920 | tf_op jit(solution)/shard_map/ppermute | solution.py:30
  12.4 7.5 %copy-start.1 = (bf16[3,3,3,64,64]{4,3,2,1,0:T(8,128)(2,1)S(1)}, bf16[3,3,3,64,64]{4,3,2,1,0:T(8,128)(2,1)}, u32[]{:S(2)}) copy-start(bf16[3,3,3,64,64]{4,3,2,1,0:T(8,128)(2,1)} %param.7) | copy-start | bytes 663556
  12.5 3.4 %collective-permute-start.2 = (bf16[2,14,64,3]{3,2,1,0:T(8,128)(2,1)S(1)}, bf16[2,14,64,3]{3,2,1,0:T(8,128)(2,1)S(1)}, u32[]{:S(2)}, u32[]{:S(2)}) collective-permute-start(bf16[2,14,64,3]{3,2,1,0:T(8,128)(2,1)S(1)} %get-tuple-element.9), channel_id=1, source_target_pairs={{0,1},{1,2},{2,3},{3,4},{4,5},{5,6},{6,7},{7,8},{8,9},{9,10},{10,1... | collective-permute-start | bytes 32264 | tf_op jit(solution)/shard_map/ppermute | solution.py:29
  13.9 5.5 %collective-permute-start.3 = (bf16[2,14,64,3]{3,2,1,0:T(8,128)(2,1)S(1)}, bf16[2,14,64,3]{3,2,1,0:T(8,128)(2,1)S(1)}, u32[]{:S(2)}, u32[]{:S(2)}) collective-permute-start(bf16[2,14,64,3]{3,2,1,0:T(8,128)(2,1)S(1)} %get-tuple-element.10), channel_id=1, source_target_pairs={{1,0},{2,1},{3,2},{4,3},{5,4},{6,5},{7,6},{8,7},{9,8},{10,9},{11,1... | collective-permute-start | bytes 32264 | tf_op jit(solution)/shard_map/ppermute | solution.py:30
  29.6 15.1 %copy-start.2 = (s32[8,128]{1,0:T(8,128)S(1)}, s32[8,128]{1,0:T(8,128)}, u32[]{:S(2)}) copy-start(s32[8,128]{1,0:T(8,128)} %param.9) | copy-start | bytes 12292
  30.4 14.4 %collective-permute-start.4 = (bf16[8,64,128]{2,1,0:T(8,128)(2,1)S(1)}, bf16[8,64,128]{2,1,0:T(8,128)(2,1)S(1)}, u32[]{:S(2)}, u32[]{:S(2)}) collective-permute-start(bf16[8,64,128]{2,1,0:T(8,128)(2,1)S(1)} %slice_bitcast_fusion), channel_id=1, source_target_pairs={{0,3},{1,4},{2,5},{3,6},{4,7},{5,8},{6,9},{7,10},{8,11},{9,12},{10... | collective-permute-start | bytes 393224 | tf_op jit(solution)/shard_map/ppermute | solution.py:19
  40.1 6.3 %collective-permute-start.5 = (bf16[8,64,128]{2,1,0:T(8,128)(2,1)S(1)}, bf16[8,64,128]{2,1,0:T(8,128)(2,1)S(1)}, u32[]{:S(2)}, u32[]{:S(2)}) collective-permute-start(bf16[8,64,128]{2,1,0:T(8,128)(2,1)S(1)} %slice_bitcast_fusion), channel_id=1, source_target_pairs={{0,2},{1,3},{2,4},{3,5},{4,6},{5,7},{6,8},{7,9},{8,10},{9,11},{10,... | collective-permute-start | bytes 393224 | tf_op jit(solution)/shard_map/ppermute | solution.py:19
  43.3 3.1 %collective-permute-start.6 = (bf16[8,64,128]{2,1,0:T(8,128)(2,1)S(1)}, bf16[8,64,128]{2,1,0:T(8,128)(2,1)S(1)}, u32[]{:S(2)}, u32[]{:S(2)}) collective-permute-start(bf16[8,64,128]{2,1,0:T(8,128)(2,1)S(1)} %slice_bitcast_fusion), channel_id=1, source_target_pairs={{0,1},{1,2},{2,3},{3,4},{4,5},{5,6},{6,7},{7,8},{8,9},{9,10},{10,1... | collective-permute-start | bytes 393224 | tf_op jit(solution)/shard_map/ppermute | solution.py:19
  152.5 1.1 copy-start

commit v4 on v3

--- a/solution.py
+++ b/solution.py
@@ -11,25 +11,6 @@
 SUB = 8
 PARTS = DISPARITIES // SUB
 MESH = pl.DeviceIdType.MESH
-
-
-def from_behind(block, axis, distance):
-    devices = range(lax.axis_size(axis))
-    route = [(i - distance, i) for i in devices if i - distance in devices]
-    return lax.ppermute(block, axis, route)
-
-
-def extended_2(value, sides, width):
-    for axis, dim in sides:
-        count, length = (lax.axis_size(axis), value.shape[dim])
-        up = [(i, (i + 1) % count) for i in range(count - 1)]
-        down = [(j, i) for i, j in up]
-        last = lax.slice_in_dim(value, length - width, length, axis=dim)
-        first = lax.slice_in_dim(value, 0, width, axis=dim)
-        before = lax.ppermute(last, axis, up)
-        after = lax.ppermute(first, axis, down)
-        value = jnp.concatenate([before, value, after], axis=dim)
-    return value
 
 
 def order_matrix():
@@ -378,43 +359,296 @@
     )(cost, charges)
 
 
-def conv_stack(stereo_neuron_outputs, filter_tap_coefficients, filter_stack_intercepts):
-    layers_total = filter_tap_coefficients.shape[0]
-    rows_here = stereo_neuron_outputs.shape[1]
-    cols_here = stereo_neuron_outputs.shape[3]
-    hidden = extended_2(stereo_neuron_outputs, (("row", 1), ("col", 3)), layers_total)
-    row_start = lax.axis_index("row") * rows_here
-    col_start = lax.axis_index("col") * cols_here
-    row_limit = lax.axis_size("row") * rows_here
-    col_limit = lax.axis_size("col") * cols_here
-    features = None
-    for layer_number in range(layers_total):
-        margin = layers_total - 1 - layer_number
-        out_rows = rows_here + 2 * margin
-        out_cols = cols_here + 2 * margin
-        summed = None
-        for tap_row in range(3):
-            for tap_col in range(3):
-                window = hidden[:, tap_row : tap_row + out_rows, :, tap_col : tap_col + out_cols]
-                term = jnp.einsum(
-                    "oc,iycx->iyox",
-                    filter_tap_coefficients[layer_number, tap_row, tap_col],
-                    window,
-                    preferred_element_type=jnp.float32,
+def outer_kernel_sizes(images, halo):
+    rows, channels, count = images.shape[1:]
+    return rows, channels, count, rows + 2 * halo
+
+
+def cost_kernel(
+    row_size,
+    col_size,
+    layers_total,
+    images,
+    taps,
+    biases,
+    present,
+    shift,
+    cost,
+    above,
+    below,
+    packed,
+    from_left,
+    from_right,
+    stack_a,
+    stack_b,
+    left_unit,
+    reach_unit,
+    rows_send,
+    rows_recv,
+    cols_send,
+    cols_recv,
+    unit_send,
+    unit_recv,
+):
+    rows, channels, count, tall = outer_kernel_sizes(images, layers_total)
+    far = reach_unit.shape[0] - 1
+    deep = 3 * channels
+    row, me = lax.axis_index("row"), lax.axis_index("col")
+    has_up, has_down = row > 0, row < row_size - 1
+    has_left, has_right = me > 0, me < col_size - 1
+
+    barrier = pltpu.get_barrier_semaphore()
+    expected = jnp.where(has_up, 1, 0) + jnp.where(has_down, 1, 0)
+    for there, step in ((has_up, -1), (has_down, 1)):
+
+        @pl.when(there)
+        def _(step=step):
+            pl.semaphore_signal(barrier, inc=1, device_id={"row": row + step}, device_id_type=MESH)
+
+    for distance in range(1, far + 1):
+        for there, step in ((me >= distance, -distance), (me + distance < col_size, distance)):
+            expected = expected + jnp.where(there, 1, 0)
+
+            @pl.when(there)
+            def _(step=step):
+                pl.semaphore_signal(
+                    barrier, inc=1, device_id={"col": me + step}, device_id_type=MESH
                 )
-                summed = term if summed is None else summed + term
-        summed = summed + filter_stack_intercepts[layer_number][None, None, :, None]
-        if layer_number < layers_total - 1:
-            global_rows = row_start - margin + jnp.arange(out_rows, dtype=jnp.int32)
-            global_cols = col_start - margin + jnp.arange(out_cols, dtype=jnp.int32)
-            keep_rows = jnp.logical_and(global_rows >= 0, global_rows < row_limit)
-            keep_cols = jnp.logical_and(global_cols >= 0, global_cols < col_limit)
-            keeper = jnp.logical_and(keep_rows[None, :, None, None], keep_cols[None, None, None, :])
-            hidden = jnp.where(keeper, jnp.maximum(summed, 0.0), 0.0).astype(jnp.bfloat16)
-        else:
-            features = summed
-    scale = lax.rsqrt(jnp.sum(features * features, axis=2, keepdims=True) + 1e-06)
-    return (features * scale).astype(jnp.bfloat16)
+
+    pl.semaphore_wait(barrier, expected)
+
+    def row_copy(step):
+        index = 0 if step < 0 else 1
+        first = 0 if step < 0 else rows - layers_total
+        return pltpu.make_async_remote_copy(
+            src_ref=images.at[:, first : first + layers_total],
+            dst_ref=below if step < 0 else above,
+            send_sem=rows_send.at[index],
+            recv_sem=rows_recv.at[index],
+            device_id={"row": row + step},
+            device_id_type=MESH,
+        )
+
+    def col_copy(step):
+        index = 0 if step < 0 else 1
+        return pltpu.make_async_remote_copy(
+            src_ref=packed,
+            dst_ref=from_right if step < 0 else from_left,
+            send_sem=cols_send.at[index],
+            recv_sem=cols_recv.at[index],
+            device_id={"col": me + step},
+            device_id_type=MESH,
+        )
+
+    def unit_copy(distance):
+        return pltpu.make_async_remote_copy(
+            src_ref=reach_unit.at[0],
+            dst_ref=reach_unit.at[distance],
+            send_sem=unit_send.at[distance],
+            recv_sem=unit_recv.at[distance],
+            device_id={"col": me + distance},
+            device_id_type=MESH,
+        )
+
+    pl.when(has_up)(lambda: row_copy(-1).start())
+    pl.when(has_down)(lambda: row_copy(1).start())
+
+    @pl.when(jnp.logical_not(has_up))
+    def _():
+        above[...] = jnp.zeros_like(above)
+
+    @pl.when(jnp.logical_not(has_down))
+    def _():
+        below[...] = jnp.zeros_like(below)
+
+    pl.when(has_down)(lambda: row_copy(-1).wait_recv())
+    pl.when(has_up)(lambda: row_copy(1).wait_recv())
+
+    def row_of(image, k):
+        if k < layers_total:
+            return above[image, k]
+        if k < layers_total + rows:
+            return images[image, k - layers_total]
+        return below[image, k - layers_total - rows]
+
+    pick_row = lax.broadcasted_iota(jnp.int32, (count, count), 0)
+    pick_lane = lax.broadcasted_iota(jnp.int32, (count, count), 1)
+
+    def one_hot(where):
+        return jnp.where(where, 1.0, 0.0).astype(jnp.bfloat16)
+
+    for image in range(2):
+        total = None
+        for k in range(tall):
+            slot = pick_lane - k * SUB
+            head = jnp.logical_and(slot >= 0, jnp.logical_and(slot < 3, pick_row == slot))
+            tail = jnp.logical_and(
+                slot >= 3, jnp.logical_and(slot < 6, pick_row == slot + count - 6)
+            )
+            pick = one_hot(jnp.logical_or(head, tail))
+            term = jnp.dot(row_of(image, k), pick, preferred_element_type=jnp.float32)
+            total = term if total is None else total + term
+        packed[image] = total.astype(jnp.bfloat16)
+
+    pl.when(has_left)(lambda: col_copy(-1).start())
+    pl.when(has_right)(lambda: col_copy(1).start())
+
+    @pl.when(jnp.logical_not(has_left))
+    def _():
+        from_left[...] = jnp.zeros_like(from_left)
+
+    @pl.when(jnp.logical_not(has_right))
+    def _():
+        from_right[...] = jnp.zeros_like(from_right)
+
+    for distance in range(1, far + 1):
+
+        @pl.when(me < distance)
+        def _(distance=distance):
+            reach_unit[distance] = jnp.zeros(reach_unit.shape[1:], reach_unit.dtype)
+
+    pl.when(has_right)(lambda: col_copy(-1).wait_recv())
+    pl.when(has_left)(lambda: col_copy(1).wait_recv())
+
+    lanes = lax.broadcasted_iota(jnp.int32, (channels, 2 * count), 1)
+    side = jnp.where(lanes < count + count // 2, has_right.astype(jnp.int32), has_left.astype(jnp.int32))
+    keep_lane = jnp.where(lanes < count, 1, side)
+
+    def put(stack, k, value):
+        base = k * deep if isinstance(k, int) else pl.multiple_of(k * deep, deep)
+        for b, turn in enumerate((1, 0, 2 * count - 1)):
+            moved = pltpu.roll(value, turn, 1) if turn else value
+            stack[pl.ds(base + b * channels, channels), :] = moved.astype(jnp.bfloat16)
+
+    def features(image):
+        for k in range(tall):
+            slot_left = pick_row - k * SUB - 3 == pick_lane - (count - 3)
+            slot_left = jnp.logical_and(slot_left, pick_lane >= count - 3)
+            slot_right = jnp.logical_and(pick_row - k * SUB == pick_lane, pick_lane < 3)
+            edge = jnp.dot(
+                from_left[image], one_hot(slot_left), preferred_element_type=jnp.float32
+            ) + jnp.dot(
+                from_right[image], one_hot(slot_right), preferred_element_type=jnp.float32
+            )
+            put(
+                stack_a,
+                k,
+                jnp.concatenate([row_of(image, k).astype(jnp.float32), edge], axis=1),
+            )
+        source, target = stack_a, stack_b
+        for layer_number in range(layers_total):
+            margin = layers_total - 1 - layer_number
+            bias = biases[layer_number]
+            weights = taps[layer_number]
+            last = margin == 0
+
+            def body(pair, _):
+                for k in range(2):
+                    y = pair * 2 + k
+                    window = source[pl.ds(pl.multiple_of(y * deep, deep), 3 * deep), :]
+                    if last:
+                        window = window[:, :count]
+                    value = jnp.dot(weights, window, preferred_element_type=jnp.float32) + bias
+                    if last:
+                        square = jnp.sum(value * value, axis=0, keepdims=True)
+                        unit = (value * lax.rsqrt(square + 1e-06)).astype(jnp.bfloat16)
+                        start = pl.multiple_of(y * channels, channels)
+                        if image == 1:
+                            reach_unit[0, pl.ds(start, channels), :] = unit
+                        else:
+                            left_unit[pl.ds(start, channels), :] = unit
+                    else:
+                        keep = jnp.logical_and(
+                            jnp.logical_or(y >= margin, has_up),
+                            jnp.logical_or(y < margin + rows, has_down),
+                        )
+                        value = jnp.where(
+                            keep_lane * keep.astype(jnp.int32) == 1, jnp.maximum(value, 0.0), 0.0
+                        )
+                        put(target, y, value)
+                return 0
+
+            lax.fori_loop(0, (rows + 2 * margin) // 2, body, 0)
+            source, target = target, source
+
+    features(1)
+    for distance in range(1, far + 1):
+        pl.when(me + distance < col_size)(lambda distance=distance: unit_copy(distance).start())
+    features(0)
+    for distance in range(1, far + 1):
+        pl.when(me >= distance)(lambda distance=distance: unit_copy(distance).wait_recv())
+
+    wide = (far + 1) * count
+    place = lax.broadcasted_iota(jnp.int32, (wide, 2 * count), 0)
+    lane = lax.broadcasted_iota(jnp.int32, (wide, 2 * count), 1)
+    choose = one_hot(place + lane == wide - 1 - shift[0, 0])
+
+    def match(y, _):
+        start = pl.multiple_of(y * channels, channels)
+        reach = jnp.concatenate(
+            [reach_unit[distance, pl.ds(start, channels), :] for distance in range(far, -1, -1)],
+            axis=1,
+        )
+        strip = jnp.dot(reach, choose, preferred_element_type=jnp.float32).astype(jnp.bfloat16)
+        held = present[pl.ds(y, 1), :] == 1
+        left = left_unit[pl.ds(start, channels), :].astype(jnp.float32)
+        left = jnp.where(held, left, 0.0).astype(jnp.bfloat16)
+        product = lax.dot_general(
+            left, strip, (((0,), (0,)), ((), ())), preferred_element_type=jnp.float32
+        )
+        skewed = pltpu.roll(product, count + 1, 1, stride=1, stride_axis=0)
+        cost[y] = 1.0 - skewed[:, :DISPARITIES]
+        return 0
+
+    lax.fori_loop(0, rows, match, 0)
+
+    pl.when(has_up)(lambda: row_copy(-1).wait_send())
+    pl.when(has_down)(lambda: row_copy(1).wait_send())
+    pl.when(has_left)(lambda: col_copy(-1).wait_send())
+    pl.when(has_right)(lambda: col_copy(1).wait_send())
+    for distance in range(1, far + 1):
+        pl.when(me + distance < col_size)(lambda distance=distance: unit_copy(distance).wait_send())
+
+
+def cost_call(images, taps, biases, present, shift):
+    rows, channels, count = images.shape[1:]
+    layers_total = taps.shape[0]
+    tall = rows + 2 * layers_total
+    far = (3 * count + DISPARITIES - 2) // count
+    taps = jnp.transpose(taps, (0, 3, 1, 2, 4)).reshape(layers_total, channels, 9 * channels)
+    vmem = pl.BlockSpec(memory_space=pltpu.VMEM)
+    halo = pltpu.VMEM((2, layers_total, channels, count), jnp.bfloat16)
+    edge = pltpu.VMEM((2, channels, count), jnp.bfloat16)
+    stack = pltpu.VMEM((tall * 3 * channels, 2 * count), jnp.bfloat16)
+    return pl.pallas_call(
+        functools.partial(
+            cost_kernel, lax.axis_size("row"), lax.axis_size("col"), layers_total
+        ),
+        out_shape=jax.ShapeDtypeStruct((rows, count, DISPARITIES), jnp.float32),
+        in_specs=[vmem, vmem, vmem, vmem, pl.BlockSpec(memory_space=pltpu.SMEM)],
+        out_specs=vmem,
+        scratch_shapes=[
+            halo,
+            halo,
+            edge,
+            edge,
+            edge,
+            stack,
+            stack,
+            pltpu.VMEM((rows * channels, count), jnp.bfloat16),
+            pltpu.VMEM((far + 1, rows * channels, count), jnp.bfloat16),
+            pltpu.SemaphoreType.DMA((2,)),
+            pltpu.SemaphoreType.DMA((2,)),
+            pltpu.SemaphoreType.DMA((2,)),
+            pltpu.SemaphoreType.DMA((2,)),
+            pltpu.SemaphoreType.DMA((far + 1,)),
+            pltpu.SemaphoreType.DMA((far + 1,)),
+        ],
+        compiler_params=pltpu.CompilerParams(
+            collective_id=1, has_side_effects=True, vmem_limit_bytes=60 * 1024 * 1024
+        ),
+        name="matching_cost",
+    )(images, taps, biases[:, :, None], present, shift)
 
 
 def per_device(
@@ -425,29 +659,16 @@
     tile_shift_amounts,
     smoothness_charges,
 ):
-    unit = conv_stack(stereo_neuron_outputs, filter_tap_coefficients, filter_stack_intercepts)
-    left_unit = unit[0]
-    right_normalized_features = unit[1]
-    rows_here = left_unit.shape[0]
-    cols_here = left_unit.shape[2]
-    reach = (3 * cols_here + DISPARITIES - 2) // cols_here
-    tile_offset = tile_shift_amounts[0, 0]
-    pieces = [
-        from_behind(right_normalized_features, "col", distance) for distance in range(reach, 0, -1)
-    ]
-    extended = jnp.concatenate(pieces + [right_normalized_features], axis=2)
-    strip_start = reach * cols_here - tile_offset - (DISPARITIES - 1)
-    strip = lax.dynamic_slice_in_dim(extended, strip_start, cols_here + DISPARITIES - 1, 2)
-    product = jnp.einsum("ycj,yck->yjk", left_unit, strip, preferred_element_type=jnp.float32)
-    padded = jnp.pad(product, ((0, 0), (0, 0), (0, 1)))
-    flat = padded.reshape(rows_here, cols_here * (cols_here + DISPARITIES))
-    flat = jnp.pad(flat, ((0, 0), (0, cols_here)))
-    skewed = flat.reshape(rows_here, cols_here, cols_here + DISPARITIES + 1)[:, :, :DISPARITIES]
-    similarity = skewed[:, :, ::-1]
-    cost = jnp.where(reference_picture_present[:, :, None] == 1, 1.0 - similarity, 1.0)
+    cost = cost_call(
+        stereo_neuron_outputs,
+        filter_tap_coefficients,
+        filter_stack_intercepts,
+        reference_picture_present,
+        tile_shift_amounts,
+    )
     across, down = paths_call(cost, smoothness_charges)
-    down = down.reshape(lax.axis_size("row"), rows_here, -1, DISPARITIES).astype(jnp.float32)
-    down = jnp.swapaxes(down, 0, 1).reshape(cost.shape)
+    down = down.reshape(lax.axis_size("row"), cost.shape[0], -1, DISPARITIES)
+    down = jnp.swapaxes(down.astype(jnp.float32), 0, 1).reshape(cost.shape)
     return down + jnp.swapaxes(across, 0, 1)
 
 

time: 155 us -> 138 us (0.89)
  the two profiles are of different devices: /device:TPU:66 before, /device:TPU:32 now
where the time goes in v4:
time: 138 us
  Pallas kernels  130 us (94%)
  local copies, waits for them, and re-layouts  5.49 us (4%)
    pallas_call x1, Pallas kernels, paths_call(): pl.pallas_call(functools.partial(paths_kernel, row_size, col_size), out_s...  104 us
    pallas_call x1, Pallas kernels, cost_call(): pl.pallas_call(functools.partial(cost_kernel, lax.axis_size('row'), lax.a...  26.5 us

profile of v4, /device:TPU:32, one launch (start us, length us, event | category | flops | bytes accessed | tf_op | source)
XLA Modules:
  0.0 137.5 jit_solution(8354959038768888800)
XLA Ops:
  0.7 0.0 copy-start.1
  0.7 0.7 copy-done.1
  1.3 0.8 copy.12.biases
  2.1 1.3 copy.10
  3.3 0.9 copy.11.taps
  4.2 26.5 %matching_cost.1.cost = f32[8,128,128]{2,1,0:T(8,128)} custom-call(bf16[2,8,64,128]{3,2,1,0:T(8,128)(2,1)} %images.1, bf16[3,64,576]{2,1,0:T(8,128)(2,1)} %copy.11.taps, f32[3,64,1]{2,1,0:T(8,128)} %copy.12.biases, s32[8,128]{1,0:T(8,128)} %present.1, s32[1,1]{1,0:T(1,128)S(6)} %copy.15.shift), custom_call_target="tpu_custom_call" | custom-call | tf_op jit(solution)/shard_map/matching_cost/pallas_call | solution.py:623
  30.7 103.8 %four_paths.1 = (f32[128,8,128]{2,1,0:T(8,128)}, bf16[32,32,128]{2,1,0:T(8,128)(2,1)}) custom-call(f32[8,128,128]{2,1,0:T(8,128)} %matching_cost.1.cost, s32[2]{0:T(128)} %charges.1), custom_call_target="tpu_custom_call" | custom-call | tf_op jit(solution)/shard_map/four_paths/pallas_call | solution.py:328
  134.5 1.0 convert.6
  135.5 0.0 copy-start
  135.6 1.0 copy-done
  136.6 0.1 bitcast_add_fusion
  136.6 0.9 copy.14
  (1 shorter events, 0.0 us)
Async XLA Ops:
  0.7 0.7 copy-start.1
  135.5 1.0 copy-start

commit v5 on v4

--- a/solution.py
+++ b/solution.py
@@ -86,14 +86,169 @@
     return jnp.concatenate([piece - least for piece in pieces_of(walked[t])], axis=0).T
 
 
-def turn_in(piece, slots, count, order):
-    def body(turn, _):
-        for k in range(16):
-            t = turn * 16 + k
-            slots[t] = turned(piece(t), order)
-        return 0
-
-    lax.fori_loop(0, count // 16, body, 0)
+BLOCK = 16
+OFFSETS = 2 * BLOCK + 1
+TABLE = 5 * SUB + 2 * BLOCK
+
+
+def row_paths(came, back, charges, way, order, costs, table, turned_table, states):
+    tiles = came.shape[0]
+    sub = lax.broadcasted_iota(jnp.int32, (SUB, DISPARITIES), 0)
+    first_sub, last_sub = sub == 0, sub == SUB - 1
+    p1 = charges[0].astype(jnp.float32) / 64.0
+    p2 = charges[1].astype(jnp.float32) / 64.0
+    middle = DISPARITIES
+
+    def at(n):
+        return jnp.where(way == 0, n, BLOCK - 1 - n)
+
+    def take(pair, _):
+        start = pl.multiple_of(pair * 2 * SUB, 2 * SUB)
+        parts = [came[c, pl.ds(start, 2 * SUB), :].astype(jnp.float32) for c in range(tiles)]
+        for half in range(2):
+            rows = [part[half * SUB : (half + 1) * SUB] for part in parts]
+            value = turned(jnp.concatenate(rows, axis=0), order)
+            for v, piece in enumerate(pieces_of(value)):
+                t = pair * 2 + half
+                lower = jnp.where(first_sub, jnp.inf, pltpu.roll(piece, 1, 0))
+                upper = jnp.where(last_sub, jnp.inf, pltpu.roll(piece, SUB - 1, 0))
+                costs[t, v * SUB : (v + 1) * SUB, :] = lower
+                costs[t, middle + v * SUB : middle + (v + 1) * SUB, :] = piece
+                costs[t, 2 * middle + v * SUB : 2 * middle + (v + 1) * SUB, :] = upper
+        return 0
+
+    lax.fori_loop(0, BLOCK // 2, take, 0)
+
+    def keep(index, v, value):
+        table[index, pl.ds(pl.multiple_of(v * SUB, SUB), SUB), :] = value
+
+    def no_jump(v, _):
+        paths = {0: None}
+        for n in range(BLOCK):
+            t = at(n)
+            fresh = {}
+            for o in range(-n - 1, n + 2):
+                near = [paths[q] for q in (o - 1, o + 1) if q in paths]
+                start = pl.multiple_of((PARTS + v + o) * SUB, SUB)
+                cost = costs[t, pl.ds(start, SUB), :]
+                if n == 0:
+                    fresh[o] = cost if o == 0 else cost + p1
+                    continue
+                best = near[0] if len(near) == 1 else jnp.minimum(near[0], near[1])
+                best = best + p1
+                if o in paths:
+                    best = jnp.minimum(paths[o], best)
+                fresh[o] = cost + best
+            paths = fresh
+            if n < BLOCK - 1:
+                level = list(paths.values())
+                while len(level) > 1:
+                    rest = level[len(level) // 2 * 2 :]
+                    level = [
+                        jnp.minimum(level[2 * i], level[2 * i + 1]) for i in range(len(level) // 2)
+                    ] + rest
+                keep(5 * SUB + n + 1, v, level[0])
+        for o in range(-BLOCK, BLOCK + 1):
+            keep(BLOCK + o, v, paths[o])
+        for index in range(OFFSETS, 5 * SUB):
+            keep(index, v, jnp.full((SUB, DISPARITIES), jnp.inf, jnp.float32))
+        keep(5 * SUB, v, jnp.zeros((SUB, DISPARITIES), jnp.float32))
+        return 0
+
+    lax.fori_loop(0, PARTS, no_jump, 0)
+
+    def costs_of(n):
+        t = at(n)
+        return [costs[t, middle + v * SUB : middle + (v + 1) * SUB, :] for v in range(PARTS)]
+
+    def jumped(first, _):
+        def one(n, state):
+            return tuple(step_once(list(state), costs_of(n), p1, p2, first_sub, last_sub)[0])
+
+        state = lax.fori_loop(first + 1, BLOCK, one, tuple(costs_of(first)))
+        for v in range(PARTS):
+            table[5 * SUB + BLOCK + first, v * SUB : (v + 1) * SUB, :] = state[v] + p2
+        return 0
+
+    lax.fori_loop(0, BLOCK, jumped, 0)
+
+    def turn(group, _):
+        for k in range(4):
+            turned_table[group * 4 + k] = table[group * 4 + k].T
+        return 0
+
+    lax.fori_loop(0, TABLE // 4, turn, 0)
+    lane = lax.broadcasted_iota(jnp.int32, (SUB, DISPARITIES), 1)
+    natural = (lane % PARTS) * SUB + lane // PARTS
+
+    def sort(group, _):
+        for k in range(8):
+            for v in range(PARTS):
+                piece = turned_table[group * 8 + k, v * SUB : (v + 1) * SUB, :]
+                turned_table[group * 8 + k, v * SUB : (v + 1) * SUB, :] = jnp.take_along_axis(
+                    piece, natural, axis=1
+                )
+        return 0
+
+    lax.fori_loop(0, TABLE // 8, sort, 0)
+
+    def apply(turn_of, state):
+        for k in range(SUB):
+            n = turn_of * SUB + k
+            b = jnp.where(way == 0, n, DISPARITIES - 1 - n)
+            states[pl.ds(b, 1), :] = state[:1]
+            found = []
+            for g in range(5):
+                term = state + turned_table[g * SUB : (g + 1) * SUB, b, :]
+                amount = (g * SUB - BLOCK) % DISPARITIES
+                found.append(pltpu.roll(term, amount, 1, stride=1, stride_axis=0))
+            for g in range(2):
+                start = 5 * SUB + g * SUB
+                least = jnp.min(
+                    state + turned_table[start : start + SUB, b, :], axis=1, keepdims=True
+                )
+                start = start + BLOCK
+                found.append(least + turned_table[start : start + SUB, b, :])
+            while len(found) > 1:
+                rest = found[len(found) // 2 * 2 :]
+                found = [
+                    jnp.minimum(found[2 * i], found[2 * i + 1]) for i in range(len(found) // 2)
+                ] + rest
+            state = found[0]
+            for step in (4, 2, 1):
+                state = jnp.minimum(state, pltpu.roll(state, step, 0))
+        return state - jnp.min(state, axis=1, keepdims=True)
+
+    lax.fori_loop(
+        0, DISPARITIES // SUB, apply, jnp.zeros((SUB, DISPARITIES), jnp.float32)
+    )
+    before = states[...]
+    before = before - jnp.min(before, axis=1, keepdims=True)
+    high = before.astype(jnp.bfloat16)
+    rest = before - high.astype(jnp.float32)
+    state = pieces_of(turned(high, order) + turned(rest, order))
+
+    def inside(pair, state):
+        state = list(state)
+        results = []
+        for k in range(2):
+            state, least = step_once(
+                state, costs_of(pair * 2 + k), p1, p2, first_sub, last_sub
+            )
+            value = jnp.concatenate([piece - least for piece in state], axis=0).T
+            results.append(ordered(value.astype(jnp.bfloat16), order))
+        low = jnp.where(way == 0, results[0], results[1])
+        top = jnp.where(way == 0, results[1], results[0])
+        start = jnp.where(way == 0, pair, BLOCK // 2 - 1 - pair) * 2 * SUB
+        start = pl.multiple_of(start, 2 * SUB)
+        for c in range(tiles):
+            rows = slice(c * SUB, (c + 1) * SUB)
+            back[c, pl.ds(start, 2 * SUB), :] = jnp.concatenate(
+                [low[rows], top[rows]], axis=0
+            ).astype(jnp.bfloat16)
+        return tuple(state)
+
+    lax.fori_loop(0, BLOCK // 2, inside, tuple(state))
 
 
 def half_turn(value):
@@ -107,25 +262,30 @@
     charges,
     out_across,
     out_down,
-    slots,
-    walked,
     strips,
-    leasts,
     strip_leasts,
-    edge_out,
-    edge_in,
+    costs,
+    table,
+    turned_table,
+    states,
+    row_sent,
+    row_came,
+    row_back,
+    row_return,
     sent,
     came,
     back_out,
     back_in,
-    edge_send,
-    edge_recv,
+    row_send,
+    row_recv,
+    return_send,
+    return_recv,
     sent_sem,
     came_sem,
     back_send,
     back_recv,
 ):
-    count = out_across.shape[0]
+    rows = cost.shape[0]
     height = strips.shape[0]
     row = lax.axis_index("row")
     me = lax.axis_index("col")
@@ -133,46 +293,56 @@
     order = order_matrix()
 
     barrier = pltpu.get_barrier_semaphore()
-
-    @pl.when(me > 0)
-    def _():
-        pl.semaphore_signal(barrier, inc=1, device_id={"col": me - 1}, device_id_type=MESH)
-
-    @pl.when(me < col_size - 1)
-    def _():
-        pl.semaphore_signal(barrier, inc=1, device_id={"col": me + 1}, device_id_type=MESH)
-
-    def greet(j, _):
-        peer = lax.rem(row + j, row_size)
-        pl.semaphore_signal(barrier, inc=1, device_id={"row": peer}, device_id_type=MESH)
-        return 0
-
-    lax.fori_loop(1, row_size, greet, 0)
-
-    def exchange(source, target, send_sem, recv_sem, what):
-        def copy(mine, slot):
+    for axis, mine, size in (("row", row, row_size), ("col", me, col_size)):
+
+        def greet(j, _, axis=axis, mine=mine, size=size):
+            peer = lax.rem(mine + j, size)
+            pl.semaphore_signal(barrier, inc=1, device_id={axis: peer}, device_id_type=MESH)
+            return 0
+
+        lax.fori_loop(1, size, greet, 0)
+
+    def exchange(axis, source, target, sems, what, pick=lambda peer: peer):
+        mine, size = (row, row_size) if axis == "row" else (me, col_size)
+        send_sem, recv_sem = sems
+
+        def copy(peer, slot):
             return pltpu.make_async_remote_copy(
-                src_ref=source.at[mine],
+                src_ref=source.at[pick(peer)],
                 dst_ref=target.at[slot],
-                send_sem=send_sem.at[mine],
+                send_sem=send_sem.at[peer],
                 recv_sem=recv_sem.at[slot],
-                device_id={"row": mine},
+                device_id={axis: peer},
                 device_id_type=MESH,
             )
 
         def body(j, _):
-            peer = lax.rem(row + j, row_size)
+            peer = lax.rem(mine + j, size)
             if what == "start":
-                copy(peer, row).start()
+                copy(peer, mine).start()
             elif what == "sent":
-                copy(peer, row).wait_send()
+                copy(peer, mine).wait_send()
             else:
                 copy(peer, peer).wait_recv()
             return 0
 
-        lax.fori_loop(1, row_size, body, 0)
+        lax.fori_loop(1, size, body, 0)
         if what == "start":
-            target[row] = source[row]
+            target[mine] = source[pick(mine)]
+
+    out_rows = ("col", row_sent, row_came, (row_send, row_recv))
+    back_rows = ("col", row_back, row_return, (return_send, return_recv))
+    out_strips = ("row", sent, came, (sent_sem, came_sem))
+    back_strips = ("row", back_out, back_in, (back_send, back_recv))
+
+    def row_of(peer):
+        return lax.rem(peer, rows)
+
+    def group(y, _):
+        row_sent[y] = ordered(order, cost[y].astype(jnp.bfloat16)).astype(jnp.bfloat16)
+        return 0
+
+    lax.fori_loop(0, rows, group, 0)
 
     def cut(tile, _):
         start = pl.multiple_of(tile * SUB, SUB)
@@ -184,13 +354,12 @@
         return 0
 
     lax.fori_loop(0, row_size // 2, cut, 0)
-    neighbours = jnp.where(me > 0, 1, 0) + jnp.where(me < col_size - 1, 1, 0)
-    pl.semaphore_wait(barrier, neighbours + row_size - 1)
-    exchange(sent, came, sent_sem, came_sem, "start")
-    turn_in(lambda x: cost[:, x, :], slots, count, order)
+    pl.semaphore_wait(barrier, row_size + col_size - 2)
+    exchange(*out_rows, "start", row_of)
+    exchange(*out_strips, "start")
 
     def vertical_in():
-        exchange(sent, came, sent_sem, came_sem, "came")
+        exchange(*out_strips, "came")
 
         def body(source, _):
             near = came[source].astype(jnp.float32)
@@ -227,96 +396,37 @@
             return 0
 
         lax.fori_loop(0, row_size // 2, body, 0)
-        exchange(back_out, back_in, back_send, back_recv, "start")
-
-    def one_direction(way, first):
-        starts = me == (0 if way == 0 else col_size - 1)
-        ends = me == (col_size - 1 if way == 0 else 0)
-        toward = me + 1 if way == 0 else me - 1
-        at = (lambda t: t) if way == 0 else (lambda t: count - 1 - t)
-
-        def copy():
-            return pltpu.make_async_remote_copy(
-                src_ref=edge_out.at[way],
-                dst_ref=edge_in.at[way],
-                send_sem=edge_send.at[way],
-                recv_sem=edge_recv.at[way],
-                device_id={"col": toward},
-                device_id_type=MESH,
-            )
-
-        @pl.when(starts)
-        def _():
-            edge_in[way] = jnp.zeros((DISPARITIES, SUB), jnp.float32)
-
-        @pl.when(jnp.logical_not(starts))
-        def _():
-            copy().wait_recv()
-
-        state, least = walk(
-            slots, walked, leasts, count, pieces_of(edge_in[way]), charges, at
-        )
-
-        @pl.when(jnp.logical_not(ends))
-        def _():
-            edge_out[way] = jnp.concatenate([piece - least for piece in state], axis=0)
-            copy().start()
-
-        def body(turn, _):
-            start = turn * 16
-            results = [layer(walked, leasts, start + k) for k in range(16)]
-            if first:
-                for k in range(16):
-                    out_across[start + k] = results[k]
-            else:
-                total = [out_across[start + k] + results[k] for k in range(16)]
-                total = jnp.concatenate(total, axis=0)
-                high = total.astype(jnp.bfloat16)
-                rest = (total - high.astype(jnp.float32)).astype(jnp.bfloat16)
-                total = ordered(high, order) + ordered(rest, order)
-                for k in range(16):
-                    out_across[start + k] = total[k * SUB : (k + 1) * SUB]
-            return 0
-
-        lax.fori_loop(0, count // 16, body, 0)
-
-        @pl.when(jnp.logical_not(ends))
-        def _():
-            copy().wait_send()
-
-    place = jnp.minimum(me, col_size - 1 - me)
-    pieces = ((vertical_in, 3), (vertical_walk, 5), (vertical_out, 6))
-    for piece, threshold in pieces:
-        pl.when(place >= threshold)(piece)
-
-    @pl.when(me < col_size // 2)
-    def _():
-        one_direction(0, True)
-
-    @pl.when(me >= col_size // 2)
-    def _():
-        one_direction(1, True)
-
-    for piece, threshold in pieces:
-        pl.when(place < threshold)(piece)
-
-    @pl.when(me < col_size // 2)
-    def _():
-        one_direction(1, False)
-
-    @pl.when(me >= col_size // 2)
-    def _():
-        one_direction(0, False)
-
-    exchange(back_out, back_in, back_send, back_recv, "came")
+        exchange(*back_strips, "start")
+
+    exchange(*out_rows, "came", row_of)
+    way = me // rows
+    row_paths(row_came, row_back, charges, way, order, costs, table, turned_table, states)
+    exchange(*back_rows, "start")
+    vertical_in()
+    vertical_walk()
+    vertical_out()
+    exchange(*back_rows, "came")
+    place = lax.broadcasted_iota(jnp.int32, (DISPARITIES, DISPARITIES), 0)
+    lane = lax.broadcasted_iota(jnp.int32, (DISPARITIES, DISPARITIES), 1)
+    spread = place == (lane % SUB) * PARTS + lane // SUB
+    spread = jnp.where(spread, 1.0, 0.0).astype(jnp.bfloat16)
+
+    def gather(y, _):
+        out_across[y] = ordered(spread, row_return[y]) + ordered(spread, row_return[y + rows])
+        return 0
+
+    lax.fori_loop(0, rows, gather, 0)
+    exchange(*back_strips, "came")
 
     def hand_over(j, _):
         out_down[j] = back_in[j]
         return 0
 
     lax.fori_loop(0, row_size, hand_over, 0)
-    exchange(sent, came, sent_sem, came_sem, "sent")
-    exchange(back_out, back_in, back_send, back_recv, "sent")
+    exchange(*out_rows, "sent", row_of)
+    exchange(*back_rows, "sent")
+    exchange(*out_strips, "sent")
+    exchange(*back_strips, "sent")
 
 
 def paths_call(cost, charges):
@@ -328,25 +438,30 @@
     return pl.pallas_call(
         functools.partial(paths_kernel, row_size, col_size),
         out_shape=(
-            jax.ShapeDtypeStruct((count, rows, DISPARITIES), jnp.float32),
+            jax.ShapeDtypeStruct(cost.shape, jnp.float32),
             jax.ShapeDtypeStruct(block, jnp.bfloat16),
         ),
         in_specs=[vmem, pl.BlockSpec(memory_space=pltpu.SMEM)],
         out_specs=(vmem, vmem),
         scratch_shapes=[
-            pltpu.VMEM((count, DISPARITIES, SUB), jnp.float32),
-            pltpu.VMEM((count, DISPARITIES, SUB), jnp.float32),
             pltpu.VMEM((rows * row_size, DISPARITIES, SUB), jnp.float32),
-            pltpu.VMEM((count, SUB, SUB), jnp.float32),
             pltpu.VMEM((rows * row_size, SUB, SUB), jnp.float32),
-            pltpu.VMEM((2, DISPARITIES, SUB), jnp.float32),
-            pltpu.VMEM((2, DISPARITIES, SUB), jnp.float32),
+            pltpu.VMEM((BLOCK, 3 * DISPARITIES, DISPARITIES), jnp.float32),
+            pltpu.VMEM((TABLE, DISPARITIES, DISPARITIES), jnp.float32),
+            pltpu.VMEM((TABLE, DISPARITIES, DISPARITIES), jnp.float32),
+            pltpu.VMEM((DISPARITIES, DISPARITIES), jnp.float32),
+            pltpu.VMEM((rows, count, DISPARITIES), jnp.bfloat16),
+            pltpu.VMEM((col_size, count, DISPARITIES), jnp.bfloat16),
+            pltpu.VMEM((col_size, count, DISPARITIES), jnp.bfloat16),
+            pltpu.VMEM((col_size, count, DISPARITIES), jnp.bfloat16),
             pltpu.VMEM(block, jnp.bfloat16),
             pltpu.VMEM(block, jnp.bfloat16),
             pltpu.VMEM(block, jnp.bfloat16),
             pltpu.VMEM(block, jnp.bfloat16),
-            pltpu.SemaphoreType.DMA((2,)),
-            pltpu.SemaphoreType.DMA((2,)),
+            pltpu.SemaphoreType.DMA((col_size,)),
+            pltpu.SemaphoreType.DMA((col_size,)),
+            pltpu.SemaphoreType.DMA((col_size,)),
+            pltpu.SemaphoreType.DMA((col_size,)),
             pltpu.SemaphoreType.DMA((row_size,)),
             pltpu.SemaphoreType.DMA((row_size,)),
             pltpu.SemaphoreType.DMA((row_size,)),
@@ -669,7 +784,7 @@
     across, down = paths_call(cost, smoothness_charges)
     down = down.reshape(lax.axis_size("row"), cost.shape[0], -1, DISPARITIES)
     down = jnp.swapaxes(down.astype(jnp.float32), 0, 1).reshape(cost.shape)
-    return down + jnp.swapaxes(across, 0, 1)
+    return down + across
 
 
 def solution(mesh):

time: 138 us -> 133 us (0.964)
  the two profiles are of different devices: /device:TPU:32 before, /device:TPU:29 now
where the time goes in v5:
time: 133 us
  Pallas kernels  125 us (94%)
  local copies, waits for them, and re-layouts  4.6 us (3%)
  other arithmetic  1.85 us (1%)
    pallas_call x1, Pallas kernels, paths_call(): pl.pallas_call(functools.partial(paths_kernel, row_size, col_size), out_s...  96.9 us
    pallas_call x1, Pallas kernels, cost_call(): pl.pallas_call(functools.partial(cost_kernel, lax.axis_size('row'), lax.a...  28.5 us

profile of v5, /device:TPU:29, one launch (start us, length us, event | category | flops | bytes accessed | tf_op | source)
XLA Modules:
  0.0 132.5 jit_solution(904588056069171971)
XLA Ops:
  0.7 0.0 copy-start.1
  0.7 0.7 copy-done.1
  1.3 0.8 copy.11.biases
  2.1 1.3 copy.9
  3.3 0.9 copy.10.taps
  4.2 28.5 %matching_cost.1.cost = f32[8,128,128]{2,1,0:T(8,128)} custom-call(bf16[2,8,64,128]{3,2,1,0:T(8,128)(2,1)} %images.1, bf16[3,64,576]{2,1,0:T(8,128)(2,1)} %copy.10.taps, f32[3,64,1]{2,1,0:T(8,128)} %copy.11.biases, s32[8,128]{1,0:T(8,128)} %present.1, s32[1,1]{1,0:T(1,128)S(6)} %copy.13.shift), custom_call_target="tpu_custom_call" | custom-call | tf_op jit(solution)/shard_map/matching_cost/pallas_call | solution.py:738
  32.7 96.9 %four_paths.1 = (f32[8,128,128]{2,1,0:T(8,128)}, bf16[32,32,128]{2,1,0:T(8,128)(2,1)}) custom-call(f32[8,128,128]{2,1,0:T(8,128)} %matching_cost.1.cost, s32[2]{0:T(128)} %charges.1), custom_call_target="tpu_custom_call" | custom-call | tf_op jit(solution)/shard_map/four_paths/pallas_call | solution.py:438
  129.6 1.0 convert.6
  130.6 0.0 copy-start
  130.7 0.1 copy.12
  130.8 0.9 copy-done
  131.7 0.8 add.3
Async XLA Ops:
  0.7 0.7 copy-start.1
  130.6 1.0 copy-start

commit v6 on v5

--- a/solution.py
+++ b/solution.py
@@ -271,6 +271,8 @@
     row_sent,
     row_came,
     row_back,
+    swapped,
+    summed,
     row_return,
     sent,
     came,
@@ -278,6 +280,10 @@
     back_in,
     row_send,
     row_recv,
+    pass_send,
+    pass_recv,
+    swap_send,
+    swap_recv,
     return_send,
     return_recv,
     sent_sem,
@@ -302,41 +308,77 @@
 
         lax.fori_loop(1, size, greet, 0)
 
-    def exchange(axis, source, target, sems, what, pick=lambda peer: peer):
-        mine, size = (row, row_size) if axis == "row" else (me, col_size)
-        send_sem, recv_sem = sems
-
-        def copy(peer, slot):
-            return pltpu.make_async_remote_copy(
-                src_ref=source.at[pick(peer)],
-                dst_ref=target.at[slot],
-                send_sem=send_sem.at[peer],
-                recv_sem=recv_sem.at[slot],
-                device_id={axis: peer},
-                device_id_type=MESH,
-            )
-
+    core = lax.rem(me, 2)
+    pair, pairs = me // 2, col_size // 2
+    partner = me + 1 - 2 * core
+
+    def remote(source, target, send_sem, recv_sem, axis, peer):
+        return pltpu.make_async_remote_copy(
+            src_ref=source,
+            dst_ref=target,
+            send_sem=send_sem,
+            recv_sem=recv_sem,
+            device_id={axis: peer},
+            device_id_type=MESH,
+        )
+
+    def rows_out(there, slot):
+        peer = 2 * there + core
+        return remote(
+            row_sent.at[there],
+            row_came.at[2 * slot + core],
+            row_send.at[there],
+            row_recv.at[slot],
+            "col",
+            peer,
+        )
+
+    def rows_pass(h, side):
+        block = row_came.at[2 * h + side]
+        return remote(block, block, pass_send.at[h], pass_recv.at[h], "col", partner)
+
+    def rows_swap(h):
+        source = row_back.at[2 * h + 1 - core]
+        return remote(source, swapped.at[h], swap_send.at[h], swap_recv.at[h], "col", partner)
+
+    def rows_back(there, slot):
+        return remote(
+            summed.at[there],
+            row_return.at[slot],
+            return_send.at[there],
+            return_recv.at[slot],
+            "col",
+            2 * there + core,
+        )
+
+    def strips_out(there, slot):
+        return remote(
+            sent.at[there], came.at[slot], sent_sem.at[there], came_sem.at[slot], "row", there
+        )
+
+    def strips_back(there, slot):
+        return remote(
+            back_out.at[there],
+            back_in.at[slot],
+            back_send.at[there],
+            back_recv.at[slot],
+            "row",
+            there,
+        )
+
+    def each_peer(mine, size, work):
         def body(j, _):
-            peer = lax.rem(mine + j, size)
-            if what == "start":
-                copy(peer, mine).start()
-            elif what == "sent":
-                copy(peer, mine).wait_send()
-            else:
-                copy(peer, peer).wait_recv()
+            work(lax.rem(mine + j, size))
             return 0
 
         lax.fori_loop(1, size, body, 0)
-        if what == "start":
-            target[mine] = source[pick(mine)]
-
-    out_rows = ("col", row_sent, row_came, (row_send, row_recv))
-    back_rows = ("col", row_back, row_return, (return_send, return_recv))
-    out_strips = ("row", sent, came, (sent_sem, came_sem))
-    back_strips = ("row", back_out, back_in, (back_send, back_recv))
-
-    def row_of(peer):
-        return lax.rem(peer, rows)
+
+    def each(size, work):
+        def body(j, _):
+            work(j)
+            return 0
+
+        lax.fori_loop(0, size, body, 0)
 
     def group(y, _):
         row_sent[y] = ordered(order, cost[y].astype(jnp.bfloat16)).astype(jnp.bfloat16)
@@ -355,11 +397,13 @@
 
     lax.fori_loop(0, row_size // 2, cut, 0)
     pl.semaphore_wait(barrier, row_size + col_size - 2)
-    exchange(*out_rows, "start", row_of)
-    exchange(*out_strips, "start")
+    each_peer(pair, pairs, lambda there: rows_out(there, pair).start())
+    row_came[me] = row_sent[pair]
+    each_peer(row, row_size, lambda there: strips_out(there, row).start())
+    came[row] = sent[row]
 
     def vertical_in():
-        exchange(*out_strips, "came")
+        each_peer(row, row_size, lambda there: strips_out(there, there).wait_recv())
 
         def body(source, _):
             near = came[source].astype(jnp.float32)
@@ -381,7 +425,15 @@
         walk(strips, strips, strip_leasts, height, zero, charges, lambda t: t)
 
     def vertical_out():
+        def send(near):
+            for there in (near, row_size - 1 - near):
+
+                @pl.when(there != row)
+                def _(there=there):
+                    strips_back(there, row).start()
+
         def body(near, _):
+            pl.when(near > 0)(lambda: send(near - 1))
             far = row_size - 1 - near
             one = [layer(strips, strip_leasts, near * SUB + y) for y in range(SUB)]
             other = [layer(strips, strip_leasts, far * SUB + y) for y in range(SUB)]
@@ -396,37 +448,57 @@
             return 0
 
         lax.fori_loop(0, row_size // 2, body, 0)
-        exchange(*back_strips, "start")
-
-    exchange(*out_rows, "came", row_of)
-    way = me // rows
-    row_paths(row_came, row_back, charges, way, order, costs, table, turned_table, states)
-    exchange(*back_rows, "start")
+        send(row_size // 2 - 1)
+        back_in[row] = back_out[row]
+
+    rows_pass(pair, core).start()
+
+    def forward(j, _):
+        there = lax.rem(pair + pairs - j, pairs)
+        rows_out(there, there).wait_recv()
+        rows_pass(there, core).start()
+        return 0
+
+    lax.fori_loop(1, pairs, forward, 0)
+    each(pairs, lambda h: rows_pass(h, 1 - core).wait_recv())
+    row_paths(row_came, row_back, charges, core, order, costs, table, turned_table, states)
+    each(pairs, lambda h: rows_swap(h).start())
     vertical_in()
+
+    def add(h):
+        rows_swap(h).wait_recv()
+        mine = row_back[2 * h + core].astype(jnp.float32)
+        summed[h] = (mine + swapped[h].astype(jnp.float32)).astype(jnp.bfloat16)
+
+    each(pairs, add)
+    each_peer(pair, pairs, lambda there: rows_back(there, pair).start())
+    row_return[pair] = summed[pair]
     vertical_walk()
     vertical_out()
-    exchange(*back_rows, "came")
+    each_peer(pair, pairs, lambda there: rows_back(there, there).wait_recv())
     place = lax.broadcasted_iota(jnp.int32, (DISPARITIES, DISPARITIES), 0)
     lane = lax.broadcasted_iota(jnp.int32, (DISPARITIES, DISPARITIES), 1)
     spread = place == (lane % SUB) * PARTS + lane // SUB
     spread = jnp.where(spread, 1.0, 0.0).astype(jnp.bfloat16)
 
     def gather(y, _):
-        out_across[y] = ordered(spread, row_return[y]) + ordered(spread, row_return[y + rows])
+        out_across[y] = ordered(spread, row_return[y])
         return 0
 
     lax.fori_loop(0, rows, gather, 0)
-    exchange(*back_strips, "came")
+    each_peer(row, row_size, lambda there: strips_back(there, there).wait_recv())
 
     def hand_over(j, _):
         out_down[j] = back_in[j]
         return 0
 
     lax.fori_loop(0, row_size, hand_over, 0)
-    exchange(*out_rows, "sent", row_of)
-    exchange(*back_rows, "sent")
-    exchange(*out_strips, "sent")
-    exchange(*back_strips, "sent")
+    each_peer(pair, pairs, lambda there: rows_out(there, pair).wait_send())
+    each(pairs, lambda h: rows_pass(h, core).wait_send())
+    each(pairs, lambda h: rows_swap(h).wait_send())
+    each_peer(pair, pairs, lambda there: rows_back(there, pair).wait_send())
+    each_peer(row, row_size, lambda there: strips_out(there, row).wait_send())
+    each_peer(row, row_size, lambda there: strips_back(there, row).wait_send())
 
 
 def paths_call(cost, charges):
@@ -453,15 +525,21 @@
             pltpu.VMEM((rows, count, DISPARITIES), jnp.bfloat16),
             pltpu.VMEM((col_size, count, DISPARITIES), jnp.bfloat16),
             pltpu.VMEM((col_size, count, DISPARITIES), jnp.bfloat16),
-            pltpu.VMEM((col_size, count, DISPARITIES), jnp.bfloat16),
+            pltpu.VMEM((rows, count, DISPARITIES), jnp.bfloat16),
+            pltpu.VMEM((rows, count, DISPARITIES), jnp.bfloat16),
+            pltpu.VMEM((rows, count, DISPARITIES), jnp.bfloat16),
             pltpu.VMEM(block, jnp.bfloat16),
             pltpu.VMEM(block, jnp.bfloat16),
             pltpu.VMEM(block, jnp.bfloat16),
             pltpu.VMEM(block, jnp.bfloat16),
-            pltpu.SemaphoreType.DMA((col_size,)),
-            pltpu.SemaphoreType.DMA((col_size,)),
-            pltpu.SemaphoreType.DMA((col_size,)),
-            pltpu.SemaphoreType.DMA((col_size,)),
+            pltpu.SemaphoreType.DMA((rows,)),
+            pltpu.SemaphoreType.DMA((rows,)),
+            pltpu.SemaphoreType.DMA((rows,)),
+            pltpu.SemaphoreType.DMA((rows,)),
+            pltpu.SemaphoreType.DMA((rows,)),
+            pltpu.SemaphoreType.DMA((rows,)),
+            pltpu.SemaphoreType.DMA((rows,)),
+            pltpu.SemaphoreType.DMA((rows,)),
             pltpu.SemaphoreType.DMA((row_size,)),
             pltpu.SemaphoreType.DMA((row_size,)),
             pltpu.SemaphoreType.DMA((row_size,)),

time: 133 us -> 122 us (0.917)
  the two profiles are of different devices: /device:TPU:29 before, /device:TPU:66 now
where the time goes in v6:
time: 122 us; the launch traced here: 121 us
  Pallas kernels  114 us (93%)
  local copies, waits for them, and re-layouts  4.6 us (4%)
  other arithmetic  1.85 us (2%)
    pallas_call x1, Pallas kernels, paths_call(): pl.pallas_call(functools.partial(paths_kernel, row_size, col_size), out_s...  89 us
    pallas_call x1, Pallas kernels, cost_call(): pl.pallas_call(functools.partial(cost_kernel, lax.axis_size('row'), lax.a...  25.3 us

profile of v6, /device:TPU:66, one launch (start us, length us, event | category | flops | bytes accessed | tf_op | source)
XLA Modules:
  0.0 121.5 jit_solution(12077161365602016124)
XLA Ops:
  0.7 0.0 copy-start.1
  0.7 0.7 copy-done.1
  1.3 0.8 copy.11.biases
  2.1 1.3 %copy.9 = bf16[3,64,3,3,64]{1,4,3,2,0:T(8,128)(2,1)S(1)} copy(bf16[3,64,3,3,64]{4,1,3,2,0:T(8,128)(2,1)} %bitcast.13) | data formatting | bytes 442368 | tf_op jit(solution)/shard_map/transpose | solution.py:811
  3.3 0.9 copy.10.taps
  4.2 25.3 %matching_cost.1.cost = f32[8,128,128]{2,1,0:T(8,128)} custom-call(bf16[2,8,64,128]{3,2,1,0:T(8,128)(2,1)} %images.1, bf16[3,64,576]{2,1,0:T(8,128)(2,1)} %copy.10.taps, f32[3,64,1]{2,1,0:T(8,128)} %copy.11.biases, s32[8,128]{1,0:T(8,128)} %present.1, s32[1,1]{1,0:T(1,128)S(6)} %copy.13.shift), custom_call_target="tpu_custom_call" | custom-call | tf_op jit(solution)/shard_map/matching_cost/pallas_call | solution.py:816
  29.5 89.0 %four_paths.1 = (f32[8,128,128]{2,1,0:T(8,128)}, bf16[32,32,128]{2,1,0:T(8,128)(2,1)}) custom-call(f32[8,128,128]{2,1,0:T(8,128)} %matching_cost.1.cost, s32[2]{0:T(128)} %charges.1), custom_call_target="tpu_custom_call" | custom-call | tf_op jit(solution)/shard_map/four_paths/pallas_call | solution.py:510
  118.6 1.0 convert.6
  119.6 0.0 copy-start
  119.6 0.1 copy.12
  119.7 0.9 copy-done
  120.6 0.8 add.3
Async XLA Ops:
  0.7 0.7 copy-start.1
  119.6 1.0 copy-start

commit v7 on v6

--- a/solution.py
+++ b/solution.py
@@ -198,10 +198,6 @@
             b = jnp.where(way == 0, n, DISPARITIES - 1 - n)
             states[pl.ds(b, 1), :] = state[:1]
             found = []
-            for g in range(5):
-                term = state + turned_table[g * SUB : (g + 1) * SUB, b, :]
-                amount = (g * SUB - BLOCK) % DISPARITIES
-                found.append(pltpu.roll(term, amount, 1, stride=1, stride_axis=0))
             for g in range(2):
                 start = 5 * SUB + g * SUB
                 least = jnp.min(
@@ -209,6 +205,11 @@
                 )
                 start = start + BLOCK
                 found.append(least + turned_table[start : start + SUB, b, :])
+            for g in range(5):
+                term = state + turned_table[g * SUB : (g + 1) * SUB, b, :]
+                amount = (g * SUB - BLOCK) % DISPARITIES
+                found.append(pltpu.roll(term, amount, 1, stride=1, stride_axis=0))
+            found = found[2:] + found[:2]
             while len(found) > 1:
                 rest = found[len(found) // 2 * 2 :]
                 found = [
@@ -260,8 +261,7 @@
     col_size,
     cost,
     charges,
-    out_across,
-    out_down,
+    out,
     strips,
     strip_leasts,
     costs,
@@ -399,8 +399,6 @@
     pl.semaphore_wait(barrier, row_size + col_size - 2)
     each_peer(pair, pairs, lambda there: rows_out(there, pair).start())
     row_came[me] = row_sent[pair]
-    each_peer(row, row_size, lambda there: strips_out(there, row).start())
-    came[row] = sent[row]
 
     def vertical_in():
         each_peer(row, row_size, lambda there: strips_out(there, there).wait_recv())
@@ -460,6 +458,8 @@
         return 0
 
     lax.fori_loop(1, pairs, forward, 0)
+    each_peer(row, row_size, lambda there: strips_out(there, row).start())
+    came[row] = sent[row]
     each(pairs, lambda h: rows_pass(h, 1 - core).wait_recv())
     row_paths(row_came, row_back, charges, core, order, costs, table, turned_table, states)
     each(pairs, lambda h: rows_swap(h).start())
@@ -482,17 +482,25 @@
     spread = jnp.where(spread, 1.0, 0.0).astype(jnp.bfloat16)
 
     def gather(y, _):
-        out_across[y] = ordered(spread, row_return[y])
+        out[y] = ordered(spread, row_return[y])
         return 0
 
     lax.fori_loop(0, rows, gather, 0)
     each_peer(row, row_size, lambda there: strips_back(there, there).wait_recv())
 
-    def hand_over(j, _):
-        out_down[j] = back_in[j]
-        return 0
-
-    lax.fori_loop(0, row_size, hand_over, 0)
+    def hand_over(tile, _):
+        start = pl.multiple_of(tile * SUB, SUB)
+        near = back_in[2 * tile].astype(jnp.float32)
+        far = back_in[2 * tile + 1].astype(jnp.float32)
+        for y in range(0, SUB, 2):
+            a = near[y // 2 * SUB : (y // 2 + 1) * SUB]
+            b = far[y // 2 * SUB : (y // 2 + 1) * SUB]
+            here = pl.ds(start, SUB)
+            out[y, here, :] = out[y, here, :] + jnp.where(low, a, half_turn(b))
+            out[y + 1, here, :] = out[y + 1, here, :] + jnp.where(low, half_turn(a), b)
+        return 0
+
+    lax.fori_loop(0, row_size // 2, hand_over, 0)
     each_peer(pair, pairs, lambda there: rows_out(there, pair).wait_send())
     each(pairs, lambda h: rows_pass(h, core).wait_send())
     each(pairs, lambda h: rows_swap(h).wait_send())
@@ -509,12 +517,9 @@
     vmem = pl.BlockSpec(memory_space=pltpu.VMEM)
     return pl.pallas_call(
         functools.partial(paths_kernel, row_size, col_size),
-        out_shape=(
-            jax.ShapeDtypeStruct(cost.shape, jnp.float32),
-            jax.ShapeDtypeStruct(block, jnp.bfloat16),
-        ),
+        out_shape=jax.ShapeDtypeStruct(cost.shape, jnp.float32),
         in_specs=[vmem, pl.BlockSpec(memory_space=pltpu.SMEM)],
-        out_specs=(vmem, vmem),
+        out_specs=vmem,
         scratch_shapes=[
             pltpu.VMEM((rows * row_size, DISPARITIES, SUB), jnp.float32),
             pltpu.VMEM((rows * row_size, SUB, SUB), jnp.float32),
@@ -567,6 +572,7 @@
     present,
     shift,
     cost,
+    stacked_taps,
     above,
     below,
     packed,
@@ -654,6 +660,12 @@
     def _():
         below[...] = jnp.zeros_like(below)
 
+    for layer_number in range(layers_total):
+        for a in range(3):
+            for b in range(3):
+                first = (3 * a + b) * channels
+                stacked_taps[layer_number, :, first : first + channels] = taps[layer_number, a, b]
+
     pl.when(has_down)(lambda: row_copy(-1).wait_recv())
     pl.when(has_up)(lambda: row_copy(1).wait_recv())
 
@@ -706,6 +718,9 @@
     lanes = lax.broadcasted_iota(jnp.int32, (channels, 2 * count), 1)
     side = jnp.where(lanes < count + count // 2, has_right.astype(jnp.int32), has_left.astype(jnp.int32))
     keep_lane = jnp.where(lanes < count, 1, side)
+
+    eye = lax.broadcasted_iota(jnp.int32, (channels, channels), 0)
+    eye = eye == lax.broadcasted_iota(jnp.int32, (channels, channels), 1)
 
     def put(stack, k, value):
         base = k * deep if isinstance(k, int) else pl.multiple_of(k * deep, deep)
@@ -731,8 +746,9 @@
         source, target = stack_a, stack_b
         for layer_number in range(layers_total):
             margin = layers_total - 1 - layer_number
-            bias = biases[layer_number]
-            weights = taps[layer_number]
+            bias = jnp.broadcast_to(biases[layer_number : layer_number + 1, :], eye.shape)
+            bias = jnp.sum(jnp.where(eye, bias, 0.0), axis=1, keepdims=True)
+            weights = stacked_taps[layer_number]
             last = margin == 0
 
             def body(pair, _):
@@ -808,7 +824,6 @@
     layers_total = taps.shape[0]
     tall = rows + 2 * layers_total
     far = (3 * count + DISPARITIES - 2) // count
-    taps = jnp.transpose(taps, (0, 3, 1, 2, 4)).reshape(layers_total, channels, 9 * channels)
     vmem = pl.BlockSpec(memory_space=pltpu.VMEM)
     halo = pltpu.VMEM((2, layers_total, channels, count), jnp.bfloat16)
     edge = pltpu.VMEM((2, channels, count), jnp.bfloat16)
@@ -821,6 +836,7 @@
         in_specs=[vmem, vmem, vmem, vmem, pl.BlockSpec(memory_space=pltpu.SMEM)],
         out_specs=vmem,
         scratch_shapes=[
+            pltpu.VMEM((layers_total, channels, 9 * channels), jnp.bfloat16),
             halo,
             halo,
             edge,
@@ -841,7 +857,7 @@
             collective_id=1, has_side_effects=True, vmem_limit_bytes=60 * 1024 * 1024
         ),
         name="matching_cost",
-    )(images, taps, biases[:, :, None], present, shift)
+    )(images, taps, biases, present, shift)
 
 
 def per_device(
@@ -859,10 +875,7 @@
         reference_picture_present,
         tile_shift_amounts,
     )
-    across, down = paths_call(cost, smoothness_charges)
-    down = down.reshape(lax.axis_size("row"), cost.shape[0], -1, DISPARITIES)
-    down = jnp.swapaxes(down.astype(jnp.float32), 0, 1).reshape(cost.shape)
-    return down + across
+    return paths_call(cost, smoothness_charges)
 
 
 def solution(mesh):

time: 122 us -> 117 us (0.959)
  local copies, waits for them, and re-layouts: 4.6 us -> 1.87 us
  other arithmetic: 1.85 us -> 0 us
    transpose x1 -> x0, local copies, waits for them, and re-layouts: 1.25 us -> none  [cost_call(): jnp.transpose(taps, (0, 3, 1, 2, 4))]
where the time goes in v7:
time: 117 us
  Pallas kernels  114 us (97%)
  local copies, waits for them, and re-layouts  1.87 us (2%)
    pallas_call x1, Pallas kernels, paths_call(): pl.pallas_call(functools.partial(paths_kernel, row_size, col_size), out_s...  88.7 us
    pallas_call x1, Pallas kernels, cost_call(): pl.pallas_call(functools.partial(cost_kernel, lax.axis_size('row'), lax.a...  25.7 us

profile of v7, /device:TPU:66, one launch (start us, length us, event | category | flops | bytes accessed | tf_op | source)
XLA Modules:
  0.0 116.9 jit_solution(3241022308334012848)
XLA Ops:
  0.7 25.7 %matching_cost.1.cost = f32[8,128,128]{2,1,0:T(8,128)} custom-call(bf16[2,8,64,128]{3,2,1,0:T(8,128)(2,1)} %images.1, bf16[3,3,3,64,64]{4,3,2,1,0:T(8,128)(2,1)} %taps.1, f32[3,64]{1,0:T(4,128)} %biases.1, s32[8,128]{1,0:T(8,128)} %present.1, s32[1,1]{1,0:T(1,128)S(6)} %copy.8.shift), custom_call_target="tpu_custom_call" | custom-call | tf_op jit(solution)/shard_map/matching_cost/pallas_call | solution.py:831
  26.3 88.7 %four_paths.1 = f32[8,128,128]{2,1,0:T(8,128)} custom-call(f32[8,128,128]{2,1,0:T(8,128)} %matching_cost.1.cost, s32[2]{0:T(128)} %charges.1), custom_call_target="tpu_custom_call" | custom-call | tf_op jit(solution)/shard_map/four_paths/pallas_call | solution.py:518
  115.0 1.9 %copy.9 = f32[8,128,128]{2,1,0:T(8,128)} copy(f32[8,128,128]{2,1,0:T(8,128)} %four_paths.1) | data formatting | bytes 1048576

commit v8 on v7

--- a/solution.py
+++ b/solution.py
@@ -395,7 +395,6 @@
         sent[2 * tile + 1] = jnp.concatenate(odd, axis=0).astype(jnp.bfloat16)
         return 0
 
-    lax.fori_loop(0, row_size // 2, cut, 0)
     pl.semaphore_wait(barrier, row_size + col_size - 2)
     each_peer(pair, pairs, lambda there: rows_out(there, pair).start())
     row_came[me] = row_sent[pair]
@@ -403,20 +402,22 @@
     def vertical_in():
         each_peer(row, row_size, lambda there: strips_out(there, there).wait_recv())
 
-        def body(source, _):
-            near = came[source].astype(jnp.float32)
-            far = came[row_size - 1 - source].astype(jnp.float32)
-            for q in range(SUB // 2):
-                a = near[q * SUB : (q + 1) * SUB]
-                b = far[(3 - q) * SUB : (4 - q) * SUB]
-                first = jnp.where(low, a, b)
-                second = half_turn(jnp.where(low, b, a))
-                t = source * SUB + 2 * q
-                strips[t] = turned(first, order)
-                strips[t + 1] = turned(second, order)
+        def body(turn, _):
+            for k in range(2):
+                source = turn * 2 + k
+                near = came[source].astype(jnp.float32)
+                far = came[row_size - 1 - source].astype(jnp.float32)
+                for q in range(SUB // 2):
+                    a = near[q * SUB : (q + 1) * SUB]
+                    b = far[(3 - q) * SUB : (4 - q) * SUB]
+                    first = jnp.where(low, a, b)
+                    second = half_turn(jnp.where(low, b, a))
+                    t = source * SUB + 2 * q
+                    strips[t] = turned(first, order)
+                    strips[t + 1] = turned(second, order)
             return 0
 
-        lax.fori_loop(0, row_size, body, 0)
+        lax.fori_loop(0, row_size // 2, body, 0)
 
     def vertical_walk():
         zero = [jnp.zeros((SUB, SUB), jnp.float32) for _ in range(PARTS)]
@@ -450,6 +451,7 @@
         back_in[row] = back_out[row]
 
     rows_pass(pair, core).start()
+    lax.fori_loop(0, row_size // 2, cut, 0)
 
     def forward(j, _):
         there = lax.rem(pair + pairs - j, pairs)

time: 117 us -> 115 us (0.983)
  Pallas kernels: 114 us -> 112 us
    pallas_call x1, Pallas kernels: 88.7 us -> 86.5 us  [paths_call(): pl.pallas_call(functools.partial(paths_kernel, row_size, col_size), out_s...]
where the time goes in v8:
time: 115 us
  Pallas kernels  112 us (97%)
  local copies, waits for them, and re-layouts  1.87 us (2%)
    pallas_call x1, Pallas kernels, paths_call(): pl.pallas_call(functools.partial(paths_kernel, row_size, col_size), out_s...  86.5 us
    pallas_call x1, Pallas kernels, cost_call(): pl.pallas_call(functools.partial(cost_kernel, lax.axis_size('row'), lax.a...  25.7 us

profile of v8, /device:TPU:66, one launch (start us, length us, event | category | flops | bytes accessed | tf_op | source)
XLA Modules:
  0.0 114.7 jit_solution(12431401894862771736)
XLA Ops:
  0.7 25.7 %matching_cost.1.cost = f32[8,128,128]{2,1,0:T(8,128)} custom-call(bf16[2,8,64,128]{3,2,1,0:T(8,128)(2,1)} %images.1, bf16[3,3,3,64,64]{4,3,2,1,0:T(8,128)(2,1)} %taps.1, f32[3,64]{1,0:T(4,128)} %biases.1, s32[8,128]{1,0:T(8,128)} %present.1, s32[1,1]{1,0:T(1,128)S(6)} %copy.8.shift), custom_call_target="tpu_custom_call" | custom-call | tf_op jit(solution)/shard_map/matching_cost/pallas_call | solution.py:833
  26.3 86.5 %four_paths.1 = f32[8,128,128]{2,1,0:T(8,128)} custom-call(f32[8,128,128]{2,1,0:T(8,128)} %matching_cost.1.cost, s32[2]{0:T(128)} %charges.1), custom_call_target="tpu_custom_call" | custom-call | tf_op jit(solution)/shard_map/four_paths/pallas_call | solution.py:520
  112.8 1.9 %copy.9 = f32[8,128,128]{2,1,0:T(8,128)} copy(f32[8,128,128]{2,1,0:T(8,128)} %four_paths.1) | data formatting | bytes 1048576
